TPU v7x, 256 devices: a whole 4x4x8 slice. The times are simulated.
256 devices in a mesh: grp: 4 (over x_lo, core), cl: 64 (over x_hi, y, z).
Axes of the slice: x: 4 (x_hi: 2, x_lo: 2; x = x_hi * 2 + x_lo), y: 4, z: 8, core: 2. Of those that a mesh axis runs over, the one named last changes fastest.
Arguments:
- incident: float32 [128, 128, 512], P('cl', None, 'grp'), may hold values from -6 to 6
- near_real: float32 [128, 16, 128, 128], P('cl'), may hold values from -0.0625 to 0.0625
- near_imag: float32 [128, 16, 128, 128], P('cl'), may hold values from -0.0625 to 0.0625
- to_moments: float32 [128, 128, 128], P('cl'), may hold values from -0.5 to 0.5
- from_locals: float32 [128, 128, 128], P('cl'), may hold values from -0.25 to 0.25
- transfer_ops: float32 [16, 128, 128], replicated, may hold values from -0.09375 to 0.09375
- near_index: int32 [128, 16], P('cl'), may hold values from 0 to 5
- near_count: int32 [128], P('cl'), may hold values from 1 to 16
- cluster_box: int32 [128], P('cl'), may hold values from 0 to 1
- far_source: int32 [128, 32], P('cl'), may hold values from 0 to 127
- far_kind: int32 [128, 32], P('cl'), may hold values from 0 to 15
- far_count: int32 [128], P('cl'), may hold values from 8 to 32
Outputs:
- pressure: float32 [128, 128, 512], P('cl', None, 'grp')
- residual: float32 [128, 128, 512], P('cl', None, 'grp')
Inputs may be any that keep to these rules, and one draw needn't show every extreme that they name: `near_index`: positions 0 to 1 are the clusters of the previous slab along cl (wrapping), then this slab's, then the next slab's. `far_source`: global box numbers.
All inputs are finite; a program needn't handle non-finite values.
Results may differ from a plain program's by a relative error of at most 0.0003.
Values sent between devices are 32-bit elements; how exact they have to be, the bound alone decides.
No kernel may reach another device: no remote copies, remote signals or barrier semaphores. Data moves between devices by JAX's collectives and lax.ppermute only.
A program may use at most 64 MiB of HBM per device.

v0:
```python
import jax
import jax.numpy as jnp
from jax import lax
from jax.sharding import PartitionSpec as P

ITERS = 2


DAMPING = 0.7


def in_one_piece(arrays, axis, dim, along):
    columns = [a.reshape(*a.shape[:along], -1) for a in arrays]
    both = jnp.concatenate(columns, axis=along)
    out, at, done = (lax.all_gather(both, axis, axis=dim, tiled=True), 0, [])
    for a, column in zip(arrays, columns):
        slab = out[..., at : at + column.shape[along]]
        done.append(slab.reshape(*slab.shape[:along], *a.shape[along:]))
        at += column.shape[along]
    return tuple(done)


def partner_2(x, axis, bit):
    return lax.ppermute(x, axis, [(i, i ^ 1 << bit) for i in range(lax.axis_size(axis))])


def padded(block, sides, width):
    for axis, dim in sides:
        count = lax.axis_size(axis)
        forward = [(i, i + 1) for i in range(count - 1)]
        forward.append((count - 1, 0))
        backward = [(target, source) for source, target in forward]
        low = lax.ppermute(
            lax.slice_in_dim(block, block.shape[dim] - width, None, axis=dim), axis, forward
        )
        high = lax.ppermute(lax.slice_in_dim(block, 0, width, axis=dim), axis, backward)
        block = jnp.concatenate([low, block, high], axis=dim)
    return block


def operator_product(form, left, right):
    return jnp.einsum(form, left, right, precision=lax.Precision.HIGHEST)


def shards(
    incident,
    near_real,
    near_imag,
    to_moments,
    from_locals,
    transfer_ops,
    near_index,
    near_count,
    cluster_box,
    far_source,
    far_kind,
    far_count,
):
    per_slab, points, width = incident.shape
    box_count, far_max = far_source.shape
    kind_total, coeffs = (transfer_ops.shape[0], transfer_ops.shape[1])
    near_max = near_index.shape[1]
    parity = jnp.where(lax.axis_index("grp") < lax.axis_size("grp") // 2, -1.0, 1.0).astype(
        jnp.float32
    )
    partner_bit = lax.axis_size("grp").bit_length() - 2
    live_near = (jnp.arange(near_max, dtype=jnp.int32)[None, :] < near_count[:, None]).astype(
        jnp.float32
    )
    box_onehot_matrix = (
        cluster_box[:, None] == jnp.arange(box_count, dtype=jnp.int32)[None, :]
    ).astype(jnp.float32)
    every_source, every_kind, every_count = in_one_piece(
        (far_source, far_kind, far_count), "cl", 0, 1
    )
    total_boxes = every_source.shape[0]
    every_active = jnp.arange(far_max, dtype=jnp.int32)[None, :] < every_count[:, None]
    every_source_hot = (
        every_source[:, :, None] == jnp.arange(total_boxes, dtype=jnp.int32)[None, None, :]
    ).astype(jnp.float32)
    every_kind_hot = (
        (every_kind[:, :, None] == jnp.arange(kind_total, dtype=jnp.int32))
        & every_active[:, :, None]
    ).astype(jnp.float32)
    list_weights = operator_product("tfj,tfy->tjy", every_source_hot, every_kind_hot)
    pressure = incident
    residual = jnp.zeros_like(incident)
    for iteration in range(ITERS):
        partner = partner_2(pressure, "grp", partner_bit)
        paired = jnp.stack([pressure, parity * partner], axis=1)
        window = padded(paired, (("cl", 0),), per_slab)
        surface_panels = jnp.take(window, near_index, axis=0) * live_near[:, :, None, None, None]
        multipole_series = operator_product("cqp,cpk->cqk", to_moments, pressure)
        moment_values = operator_product("ym,ysw->msw", box_onehot_matrix, multipole_series)
        column_moments = lax.all_to_all(
            moment_values, "cl", split_axis=2, concat_axis=0, tiled=True
        )
        grouped = operator_product("tjy,jqk->tyqk", list_weights, column_moments)
        column_locals = operator_product("yrq,tyqk->trk", transfer_ops, grouped)
        local_field = lax.all_to_all(column_locals, "cl", split_axis=0, concat_axis=2, tiled=True)
        cluster_local = operator_product("cb,brk->crk", box_onehot_matrix, local_field)
        applied = (
            pressure
            + (
                operator_product("cepq,ceqk->cpk", near_real, surface_panels[:, :, 0])
                + operator_product("cepq,ceqk->cpk", near_imag, surface_panels[:, :, 1])
            )
            + operator_product("cpr,crk->cpk", from_locals, cluster_local)
        )
        residual = incident - applied
        pressure = pressure + DAMPING * residual
    return (pressure, residual)


def solution(mesh):
    return jax.shard_map(
        shards,
        mesh=mesh,
        in_specs=(
            P("cl", None, "grp"),
            P("cl", None, None, None),
            P("cl", None, None, None),
            P("cl", None, None),
            P("cl", None, None),
            P(),
            P("cl", None),
            P("cl"),
            P("cl"),
            P("cl", None),
            P("cl", None),
            P("cl"),
        ),
        out_specs=(P("cl", None, "grp"), P("cl", None, "grp")),
        check_vma=False,
    )
```

profile of v0, /device:TPU:2, one launch (start us, length us, event | category | flops | bytes accessed | tf_op | source)
XLA Modules:
  0.0 292.6 jit_solution(14853311356748450300)
XLA Ops:
  1.8 2.3 collective-permute-start
  5.5 1.8 fusion.39
  7.3 12.3 %all-to-all-start = ((f32[2,128,128]{1,0,2:T(2,128)}), f32[2,128,128]{1,0,2:T(2,128)S(1)}, u32[]{:S(2)}, u32[]{:S(2)}) async-start(f32[2,128,128]{1,0,2:T(2,128)} %fusion.39), calls=%async_computation | async-start | bytes 262144 | tf_op jit(solution)/shard_map/all_to_all | solution.py:95
  21.1 181.8 %all-gather = s32[64,2,65]{2,1,0:T(2,128)S(1)} all-gather(s32[1,2,65]{2,1,0:T(2,128)S(1)} %add_bitcast_fusion), channel_id=1, replica_groups=mesh['grp'=4,'cl'=64] {'cl'}, dimensions={0}, use_global_device_ids=true | all-gather | bytes 33800 | tf_op jit(solution)/shard_map/all_gather | solution.py:15
  204.0 2.3 fusion.4
  207.1 7.7 %collective-permute-start.2 = (f32[2,2,128,128]{2,3,0,1:T(8,128)}, f32[2,2,128,128]{2,3,0,1:T(8,128)}, u32[]{:S(2)}, u32[]{:S(2)}) collective-permute-start(f32[2,2,128,128]{2,3,0,1:T(8,128)} %pad_maximum_fusion.2), channel_id=1, source_target_pairs={{1,0},{2,1},{3,2},{4,3},{5,4},{6,5},{7,6},{8,7},{9,8},{10,9},{11,1... | collective-permute-start | bytes 786440 | tf_op jit(solution)/shard_map/ppermute | solution.py:36
  215.0 3.1 %fusion.25 = f32[128,16,128,2]{2,0,1,3:T(8,128)S(1)} fusion(f32[128,128,2,1]{1,0,3,2:T(8,128)S(1)} %bitcast.177, f32[128,128,16]{1,2,0:T(8,128)} %fusion.4), kind=kOutput, calls=%fused_computation.39 | convolution fusion | flops 805306368 | bytes 3276800 | tf_op jit(solution)/shard_map/tjy,jqk->tyqk/dot_general | solution.py:42
  218.1 1.8 convolution_bitcast_fusion.4
  220.7 4.8 %all-to-all-start.1 = ((f32[128,128,2]{1,2,0:T(2,128)}), f32[128,128,2]{1,2,0:T(2,128)S(1)}, u32[]{:S(2)}, u32[]{:S(2)}) async-start(f32[128,128,2]{1,2,0:T(2,128)} %copy.88), calls=%async_computation.1 | async-start | bytes 262144 | tf_op jit(solution)/shard_map/all_to_all | solution.py:100
  226.6 2.8 gather_fusion
  229.3 2.5 copy.78
  232.7 2.0 fusion.11
  234.8 2.1 fusion.20
  236.8 1.8 all-to-all-done.1
  239.7 1.9 collective-permute-start.3
  243.1 10.5 %all-to-all-start.2 = ((f32[2,128,128]{1,0,2:T(2,128)}), f32[2,128,128]{1,0,2:T(2,128)}, u32[]{:S(2)}, u32[]{:S(2)}) async-start(f32[2,128,128]{1,0,2:T(2,128)} %fusion.36), calls=%async_computation.2 | async-start | bytes 262144 | tf_op jit(solution)/shard_map/all_to_all | solution.py:95
  255.9 6.3 %collective-permute-start.5 = (f32[2,2,128,128]{2,3,0,1:T(8,128)}, f32[2,2,128,128]{2,3,0,1:T(8,128)}, u32[]{:S(2)}, u32[]{:S(2)}) collective-permute-start(f32[2,2,128,128]{2,3,0,1:T(8,128)} %pad_maximum_fusion.3), channel_id=1, source_target_pairs={{1,0},{2,1},{3,2},{4,3},{5,4},{6,5},{7,6},{8,7},{9,8},{10,9},{11,1... | collective-permute-start | bytes 786440 | tf_op jit(solution)/shard_map/ppermute | solution.py:36
  262.1 4.0 %all-to-all-done.2 = f32[2,128,128]{1,0,2:T(2,128)} async-done(((f32[2,128,128]{1,0,2:T(2,128)}), f32[2,128,128]{1,0,2:T(2,128)}, u32[]{:S(2)}, u32[]{:S(2)}) %all-to-all-start.2) | async-done | bytes 131104 | tf_op jit(solution)/shard_map/all_to_all | solution.py:95
  267.2 3.1 %fusion.23 = f32[128,16,128,2]{2,0,1,3:T(8,128)S(1)} fusion(f32[128,128,2,1]{1,0,3,2:T(8,128)S(1)} %bitcast.176, f32[128,128,16]{1,2,0:T(8,128)} %fusion.4), kind=kOutput, calls=%fused_computation.37 | convolution fusion | flops 805306368 | bytes 3276800 | tf_op jit(solution)/shard_map/tjy,jqk->tyqk/dot_general | solution.py:42
  272.8 4.6 %all-to-all-start.3 = ((f32[128,128,2]{1,2,0:T(2,128)}), f32[128,128,2]{1,2,0:T(2,128)S(1)}, u32[]{:S(2)}, u32[]{:S(2)}) async-start(f32[128,128,2]{1,2,0:T(2,128)} %copy.101), calls=%async_computation.3 | async-start | bytes 262144 | tf_op jit(solution)/shard_map/all_to_all | solution.py:100
  278.6 2.8 gather_fusion.1
  281.3 2.5 copy.94
  284.7 2.0 fusion.13
  286.7 2.1 fusion.17
  (70 shorter events, 22.9 us)
Async XLA Ops:
  0.6 232.0 %copy-start = (f32[2,16,128,128]{3,2,1,0:T(8,128)S(1)}, f32[2,16,128,128]{3,2,1,0:T(8,128)}, u32[]{:S(2)}) copy-start(f32[2,16,128,128]{3,2,1,0:T(8,128)} %param.15) | copy-start | bytes 6291460
  0.6 205.6 %copy-start.8 = (s32[2,16]{1,0:T(2,128)S(1)}, s32[2,16]{1,0:T(2,128)}, u32[]{:S(2)}) copy-start(s32[2,16]{1,0:T(2,128)} %param.20) | copy-start | bytes 388
  1.8 204.5 %collective-permute-start = (f32[2,128,128]{1,2,0:T(8,128)S(1)}, f32[2,128,128]{1,2,0:T(8,128)S(1)}, u32[]{:S(2)}, u32[]{:S(2)}) collective-permute-start(f32[2,128,128]{1,2,0:T(8,128)S(1)} %copy.93), channel_id=1, source_target_pairs={{0,128},{64,192},{128,0},{192,64},{1,129},{65,193},{129,1},{193,65... | collective-permute-start | bytes 393224 | tf_op jit(solution)/shard_map/ppermute | solution.py:24
  7.3 207.6 %all-to-all-start = ((f32[2,128,128]{1,0,2:T(2,128)}), f32[2,128,128]{1,0,2:T(2,128)S(1)}, u32[]{:S(2)}, u32[]{:S(2)}) async-start(f32[2,128,128]{1,0,2:T(2,128)} %fusion.39), calls=%async_computation | async-start | bytes 262144 | tf_op jit(solution)/shard_map/all_to_all | solution.py:95
  206.4 11.7 %copy-start.3 = (f32[16,128,128]{2,1,0:T(8,128)S(1)}, f32[16,128,128]{2,1,0:T(8,128)}, u32[]{:S(2)}) copy-start(f32[16,128,128]{2,1,0:T(8,128)} %param.19) | copy-start | bytes 3145732
  207.1 18.4 %collective-permute-start.1 = (f32[2,2,128,128]{2,3,0,1:T(8,128)}, f32[2,2,128,128]{2,3,0,1:T(8,128)}, u32[]{:S(2)}, u32[]{:S(2)}) collective-permute-start(f32[2,2,128,128]{2,3,0,1:T(8,128)} %pad_maximum_fusion.2), channel_id=1, source_target_pairs={{0,1},{1,2},{2,3},{3,4},{4,5},{5,6},{6,7},{7,8},{8,9},{9,10},{10,1... | collective-permute-start | bytes 786440 | tf_op jit(solution)/shard_map/ppermute | solution.py:33
  207.1 18.4 %collective-permute-start.2 = (f32[2,2,128,128]{2,3,0,1:T(8,128)}, f32[2,2,128,128]{2,3,0,1:T(8,128)}, u32[]{:S(2)}, u32[]{:S(2)}) collective-permute-start(f32[2,2,128,128]{2,3,0,1:T(8,128)} %pad_maximum_fusion.2), channel_id=1, source_target_pairs={{1,0},{2,1},{3,2},{4,3},{5,4},{6,5},{7,6},{8,7},{9,8},{10,9},{11,1... | collective-permute-start | bytes 786440 | tf_op jit(solution)/shard_map/ppermute | solution.py:36
  220.7 18.0 %all-to-all-start.1 = ((f32[128,128,2]{1,2,0:T(2,128)}), f32[128,128,2]{1,2,0:T(2,128)S(1)}, u32[]{:S(2)}, u32[]{:S(2)}) async-start(f32[128,128,2]{1,2,0:T(2,128)} %copy.88), calls=%async_computation.1 | async-start | bytes 262144 | tf_op jit(solution)/shard_map/all_to_all | solution.py:100
  232.7 2.1 copy-start.1
  234.8 4.1 %copy-start.9 = (s32[2]{0:T(128)S(1)}, s32[2]{0:T(128)}, u32[]{:S(2)}) copy-start(s32[2]{0:T(128)} %param.22) | copy-start | bytes 28
  234.8 4.5 %copy-start.6 = (f32[2,128,128]{2,1,0:T(8,128)S(1)}, f32[2,128,128]{2,1,0:T(8,128)}, u32[]{:S(2)}) copy-start(f32[2,128,128]{2,1,0:T(8,128)} %param.18) | copy-start | bytes 393220
  234.8 6.8 %copy-start.5 = (f32[2,128,128]{2,1,0:T(8,128)S(1)}, f32[2,128,128]{2,1,0:T(8,128)}, u32[]{:S(2)}) copy-start(f32[2,128,128]{2,1,0:T(8,128)} %param.17) | copy-start | bytes 393220
  239.7 14.0 %collective-permute-start.3 = (f32[2,128,128]{1,2,0:T(8,128)S(1)}, f32[2,128,128]{1,2,0:T(8,128)S(1)}, u32[]{:S(2)}, u32[]{:S(2)}) collective-permute-start(f32[2,128,128]{1,2,0:T(8,128)S(1)} %fusion.8), channel_id=1, source_target_pairs={{0,128},{64,192},{128,0},{192,64},{1,129},{65,193},{129,1},{193,65... | collective-permute-start | bytes 393224 | tf_op jit(solution)/shard_map/ppermute | solution.py:24
  243.1 23.0 %all-to-all-start.2 = ((f32[2,128,128]{1,0,2:T(2,128)}), f32[2,128,128]{1,0,2:T(2,128)}, u32[]{:S(2)}, u32[]{:S(2)}) async-start(f32[2,128,128]{1,0,2:T(2,128)} %fusion.36), calls=%async_computation.2 | async-start | bytes 262144 | tf_op jit(solution)/shard_map/all_to_all | solution.py:95
  253.7 16.6 %copy-start.4 = (f32[16,128,128]{2,1,0:T(8,128)S(1)}, f32[16,128,128]{2,1,0:T(8,128)}, u32[]{:S(2)}) copy-start(f32[16,128,128]{2,1,0:T(8,128)} %param.19) | copy-start | bytes 3145732
  254.4 23.1 %collective-permute-start.4 = (f32[2,2,128,128]{2,3,0,1:T(8,128)}, f32[2,2,128,128]{2,3,0,1:T(8,128)}, u32[]{:S(2)}, u32[]{:S(2)}) collective-permute-start(f32[2,2,128,128]{2,3,0,1:T(8,128)} %pad_maximum_fusion.3), channel_id=1, source_target_pairs={{0,1},{1,2},{2,3},{3,4},{4,5},{5,6},{6,7},{7,8},{8,9},{9,10},{10,1... | collective-permute-start | bytes 786440 | tf_op jit(solution)/shard_map/ppermute | solution.py:33
  255.9 21.6 %collective-permute-start.5 = (f32[2,2,128,128]{2,3,0,1:T(8,128)}, f32[2,2,128,128]{2,3,0,1:T(8,128)}, u32[]{:S(2)}, u32[]{:S(2)}) collective-permute-start(f32[2,2,128,128]{2,3,0,1:T(8,128)} %pad_maximum_fusion.3), channel_id=1, source_target_pairs={{1,0},{2,1},{3,2},{4,3},{5,4},{6,5},{7,6},{8,7},{9,8},{10,9},{11,1... | collective-permute-start | bytes 786440 | tf_op jit(solution)/shard_map/ppermute | solution.py:36
  272.8 17.3 %all-to-all-start.3 = ((f32[128,128,2]{1,2,0:T(2,128)}), f32[128,128,2]{1,2,0:T(2,128)S(1)}, u32[]{:S(2)}, u32[]{:S(2)}) async-start(f32[128,128,2]{1,2,0:T(2,128)} %copy.101), calls=%async_computation.3 | async-start | bytes 262144 | tf_op jit(solution)/shard_map/all_to_all | solution.py:100
  284.6 2.1 copy-start.2
  286.7 4.0 %copy-start.7 = (f32[2,128,128]{2,1,0:T(8,128)S(1)}, f32[2,128,128]{2,1,0:T(8,128)}, u32[]{:S(2)}) copy-start(f32[2,128,128]{2,1,0:T(8,128)} %param.18) | copy-start | bytes 393220
where the time goes:
time: 293 us
  blocking collectives  182 us (62%)
  starting transfers between devices  51.9 us (18%)
  matrix products  26.5 us (9%)
  local copies, waits for them, and re-layouts  17.3 us (6%)
  waiting for transfers between devices  7.11 us (2%)
  other arithmetic  7.02 us (2%)
    all_gather x1, blocking collectives, in_one_piece(): out, at, done = (lax.all_gather(both, axis, axis=dim, tiled=True), 0, [])  182 us
    dot_general x17, matrix products, operator_product(): return jnp.einsum(form, left, right, precision=lax.Precision.HIGHEST)  26.5 us
    all_to_all x2, starting transfers between devices, shards(): lax.all_to_all(moment_values, 'cl', split_axis=2, concat_axis=0, tiled=True)  22.8 us
    ppermute x2, starting transfers between devices, padded(): lax.ppermute(lax.slice_in_dim(block, 0, width, axis=dim), axis, backward)  14 us
    gather x4, local copies, waits for them, and re-layouts, shards(): jnp.take(window, near_index, axis=0) * live_near[:, :, None, None, None]  10.4 us
    all_to_all x2, starting transfers between devices, shards(): lax.all_to_all(column_locals, 'cl', split_axis=0, concat_axis=2, tiled=True)  9.42 us
  transfers between devices with their start and end apart: 10, of which 3 were waited for; matrix products, arithmetic and copies ran while one was open for 16% of the time, Pallas kernels for 0%

commit v1 on v0

v1 whole, which is shorter than its diff:
```python
import functools

import jax
import jax.numpy as jnp
from jax import lax
from jax.experimental import pallas as pl
from jax.experimental.pallas import tpu as pltpu
from jax.sharding import PartitionSpec as P

ITERS = 2
DAMPING = 0.7
F32, BF16 = jnp.float32, jnp.bfloat16
VMEM = pl.BlockSpec(memory_space=pltpu.VMEM)
SMEM = pl.BlockSpec(memory_space=pltpu.SMEM)
NT = (((1,), (1,)), ((), ()))
NN = (((1,), (0,)), ((), ()))


def halves(x):
    top = x.astype(BF16)
    return top, (x - top.astype(F32)).astype(BF16)


def dot(a, b, dims=NN):
    return lax.dot_general(a, b, dims, preferred_element_type=F32)


def product(a, b, dims=NN):
    (a0, a1), (b0, b1) = halves(a), halves(b)
    return dot(a0, b0, dims) + (dot(a0, b1, dims) + dot(a1, b0, dims))


def call(body, outs, in_specs, out_specs, name, mib=16, cycles=0, **more):
    return pl.pallas_call(
        body,
        out_shape=outs,
        in_specs=in_specs,
        out_specs=out_specs,
        name=name,
        compiler_params=pltpu.CompilerParams(vmem_limit_bytes=mib << 20),
        cost_estimate=pl.CostEstimate(flops=cycles, bytes_accessed=1 << 18, transcendentals=0),
        **more,
    )


def send_moments(field, to_moments_ref, box_ref, out_ref, rows):
    count, peers = len(field), out_ref.shape[0] // rows
    series = [product(to_moments_ref[c], field[c]).T for c in range(count)]
    for b in range(count):
        moment = sum(jnp.where(box_ref[c] == b, series[c], 0.0) for c in range(count))
        for k in range(2):
            out_ref[pl.ds(2 * b + k, peers, stride=rows), :] = moment[k * peers : (k + 1) * peers]


def first_moments_body(rows, field_ref, to_moments_ref, source_ref, kind_ref, count_ref, box_ref, out_ref):
    boxes, most = source_ref.shape
    peers = out_ref.shape[0] // rows
    at = lax.broadcasted_iota(jnp.int32, (1, most), 1)
    kinds = [jnp.where(at < count_ref[b], kind_ref[b : b + 1, :], -1) for b in range(boxes)]
    lists = jnp.concatenate([source_ref[b : b + 1, :] for b in range(boxes)] + kinds, axis=1).astype(F32)
    send_moments([field_ref[0], field_ref[1]], to_moments_ref, box_ref, out_ref, rows)
    out_ref[pl.ds(4, peers, stride=rows), :] = jnp.broadcast_to(lists, (peers, lists.shape[1]))
    for row in range(5, rows):
        out_ref[pl.ds(row, peers, stride=rows), :] = jnp.zeros((peers, lists.shape[1]), F32)


def blocks_body(index_ref, count_ref, sign_ref, real_ref, imag_ref, top_ref, rest_ref, total):
    c, part = pl.program_id(0), pl.program_id(1)
    chunk = real_ref.shape[1]

    @pl.when((c == 0) & (part == 0))
    def _():
        total[...] = jnp.zeros_like(total)

    for i in range(chunk):
        e = part * chunk + i

        @pl.when(e < count_ref[c])
        def _():
            j = index_ref[c, e]
            total[j, c, 0] += real_ref[0, i]
            total[j, c, 1] += imag_ref[0, i]

    @pl.when((c == pl.num_programs(0) - 1) & (part == pl.num_programs(1) - 1))
    def _():
        points = total.shape[3]
        for j in range(total.shape[0]):
            for cluster in range(total.shape[1]):
                for side in range(2):
                    block = total[j, cluster, side]
                    if side == 1:
                        block = block * sign_ref[0]
                    top, rest = halves(block)
                    row = (cluster * 2 + side) * points
                    here = (j // 2, pl.ds(row, points), pl.ds(j % 2 * points, points))
                    top_ref[here] = top
                    rest_ref[here] = rest


def operators_body(ops_ref, out_ref):
    size = ops_ref.shape[1]
    for y in range(ops_ref.shape[0]):
        top, rest = halves(ops_ref[y].T)
        rows = pl.ds(y % 2 * size, size)
        out_ref[y // 2, rows, 0:size] = top
        out_ref[y // 2, rows, size : 2 * size] = rest


def near_body(before_ref, own_ref, after_ref, top_ref, rest_ref, straight_ref, crossed_ref):
    points = own_ref.shape[1]
    total = None
    for slab, ref in enumerate((before_ref, own_ref, after_ref)):
        v0, v1 = halves(jnp.concatenate([ref[0], ref[1]], axis=0))
        both = dot(top_ref[slab], jnp.concatenate([v0, v1], axis=1))
        part = both[:, :points] + (both[:, points:] + dot(rest_ref[slab], v0))
        total = part if total is None else total + part
    for c in range(2):
        straight_ref[c] = total[2 * c * points : (2 * c + 1) * points]
        crossed_ref[c] = total[(2 * c + 1) * points : (2 * c + 2) * points]


def interaction_counts(in_ref, rows, counts_ref, kinds):
    peers = in_ref.shape[0] // rows
    parts = [in_ref[pl.ds(4 + rows * j, peers // 4, stride=4 * rows), :] for j in range(4)]
    lane = lax.broadcasted_iota(jnp.int32, parts[0].shape, 1)
    low = lane < 64
    turn = [pltpu.roll(p, 64, 1) for p in parts]
    source = jnp.concatenate([jnp.where(low, parts[0], turn[1]), jnp.where(low, parts[2], turn[3])], axis=1)
    kind = jnp.concatenate([jnp.where(low, turn[0], parts[1]), jnp.where(low, turn[2], parts[3])], axis=1)
    source, kind = source.astype(jnp.int32), kind.astype(jnp.int32)
    source = (source & 1) * peers + (source >> 1)
    wide = source.shape[1]
    row = lax.broadcasted_iota(jnp.int32, (2 * peers, wide), 0)
    column = lax.broadcasted_iota(jnp.int32, (2 * peers, wide), 1)
    own = (row & 7) == (column >> 5)
    for i in range(peers // 4):
        left = jnp.where(own & ((row >> 3) == kind[i : i + 1, :]), 1.0, 0.0).astype(BF16)
        right = jnp.where(row == source[i : i + 1, :], 1.0, 0.0).astype(BF16)
        block = dot(left, right, NT).astype(BF16)
        for y in range(kinds):
            counts_ref[y, 8 * i : 8 * i + 8, :] = block[8 * y : 8 * y + 8]


def transfer(in_ref, rows, ops_ref, counts_ref, out_ref):
    peers, size = in_ref.shape[0] // rows, in_ref.shape[1]
    moments = []
    for k in range(2):
        moments.append(
            jnp.concatenate([in_ref[pl.ds(2 * b + k, peers, stride=rows), :] for b in range(2)], axis=0)
        )
    m0, m1 = halves(jnp.concatenate(moments, axis=1))
    right = jnp.concatenate([m0, m1], axis=0)
    total = [None, None]
    for pair in range(ops_ref.shape[0]):
        grouped = []
        for y in (2 * pair, 2 * pair + 1):
            count = counts_ref[y]
            grouped.append(dot(jnp.concatenate([count, count], axis=1), right))
        for k in range(2):
            g0, g1 = halves(jnp.concatenate([g[:, k * size : (k + 1) * size] for g in grouped], axis=1))
            both = dot(g0, ops_ref[pair])
            part = both[:, :size] + (both[:, size:] + dot(g1, ops_ref[pair, :, :size]))
            total[k] = part if total[k] is None else total[k] + part
    for k in range(2):
        out_ref[pl.ds(k, 2 * peers, stride=2), :] = total[k]


def first_transfer_body(rows, in_ref, ops_ref, out_ref, counts_ref):
    interaction_counts(in_ref, rows, counts_ref, counts_ref.shape[0])
    transfer(in_ref, rows, ops_ref, counts_ref, out_ref)


def next_transfer_body(rows, in_ref, ops_ref, counts_ref, out_ref):
    transfer(in_ref, rows, ops_ref, counts_ref, out_ref)


def update_body(last, in_ref, from_locals_ref, to_moments_ref, box_ref, straight_ref, crossed_ref, incident_ref, pressure_ref, *outs):
    peers = in_ref.shape[0] // 4
    local = []
    for b in range(2):
        local.append(jnp.concatenate([in_ref[pl.ds(2 * b + k, peers, stride=4), :] for k in range(2)], axis=0))
    fields = []
    for c in range(2):
        far = product(from_locals_ref[c], jnp.where(box_ref[c] == 0, local[0], local[1]), NT)
        applied = pressure_ref[c] + (straight_ref[c] + crossed_ref[c]) + far
        residual = incident_ref[c] - applied
        field = pressure_ref[c] + DAMPING * residual
        fields.append(field)
        outs[0][c] = field
        if last:
            outs[1][c] = residual
    if not last:
        send_moments(fields, to_moments_ref, box_ref, outs[1], 4)


def shards(
    incident,
    near_real,
    near_imag,
    to_moments,
    from_locals,
    transfer_ops,
    near_index,
    near_count,
    cluster_box,
    far_source,
    far_kind,
    far_count,
):
    clusters, points, width = incident.shape
    near_max = near_real.shape[1]
    peers, grp = lax.axis_size("cl"), lax.axis_size("grp")
    kinds, size = transfer_ops.shape[0], transfer_ops.shape[1]
    field = jax.ShapeDtypeStruct(incident.shape, F32)
    rows = 8
    forward = [(i, (i + 1) % peers) for i in range(peers)]
    backward = [(target, source) for source, target in forward]
    across = [(i, (i + grp // 2) % grp) for i in range(grp)]
    sign = jnp.where(lax.axis_index("grp") < grp // 2, 1.0, -1.0).astype(F32).reshape(1)

    def exchange(x, pieces):
        x = x.reshape(peers, pieces, size)
        return lax.all_to_all(x, "cl", split_axis=0, concat_axis=0, tiled=True).reshape(-1, size)

    chunk = 4
    block = pl.BlockSpec((1, chunk, points, points), lambda c, part: (c, part, 0, 0))
    halved = jax.ShapeDtypeStruct((3, 4 * points, 2 * points), BF16)
    whole = pl.BlockSpec(halved.shape, lambda c, part: (0, 0, 0))
    blocks_top, blocks_rest = call(
        blocks_body,
        (halved, halved),
        [SMEM, SMEM, SMEM, block, block],
        (whole, whole),
        "neighbour_blocks",
        grid=(clusters, near_max // chunk),
        scratch_shapes=[pltpu.VMEM((6, clusters, 2, points, points), F32)],
    )(near_index, near_count, sign, near_real, near_imag)
    operators = call(
        operators_body,
        jax.ShapeDtypeStruct((kinds // 2, 2 * size, 2 * size), BF16),
        [VMEM],
        VMEM,
        "operators",
    )(transfer_ops)
    sent = call(
        functools.partial(first_moments_body, rows),
        jax.ShapeDtypeStruct((peers * rows, size), F32),
        [VMEM] * 4 + [SMEM] * 2,
        VMEM,
        "first_moments",
    )(incident, to_moments, far_source, far_kind, far_count, cluster_box)

    pressure = incident
    for iteration in range(ITERS):
        first, last = iteration == 0, iteration == ITERS - 1
        before = lax.ppermute(pressure, "cl", forward)
        after = lax.ppermute(pressure, "cl", backward)
        arrived = exchange(sent, rows if first else 4)
        straight, crossed = call(near_body, (field, field), [VMEM] * 5, (VMEM, VMEM), "near")(
            before, pressure, after, blocks_top, blocks_rest
        )
        crossed = lax.ppermute(crossed, "grp", across)
        piece = jax.ShapeDtypeStruct((peers * 4, size), F32)
        if first:
            locals_out, counts = call(
                functools.partial(first_transfer_body, rows),
                (piece, jax.ShapeDtypeStruct((kinds, 2 * peers, 2 * peers), BF16)),
                [VMEM] * 2,
                (VMEM, VMEM),
                "first_transfer",
            )(arrived, operators)
        else:
            locals_out = call(
                functools.partial(next_transfer_body, 4), piece, [VMEM] * 3, VMEM, "next_transfer"
            )(arrived, operators, counts)
        local = exchange(locals_out, 4)
        pressure, sent = call(
            functools.partial(update_body, last),
            (field, field if last else piece),
            [VMEM] * 3 + [SMEM] + [VMEM] * 4,
            (VMEM, VMEM),
            "update",
        )(local, from_locals, to_moments, cluster_box, straight, crossed, incident, pressure)
    return (pressure, sent)


def solution(mesh):
    return jax.shard_map(
        shards,
        mesh=mesh,
        in_specs=(
            P("cl", None, "grp"),
            P("cl", None, None, None),
            P("cl", None, None, None),
            P("cl", None, None),
            P("cl", None, None),
            P(),
            P("cl", None),
            P("cl"),
            P("cl"),
            P("cl", None),
            P("cl", None),
            P("cl"),
        ),
        out_specs=(P("cl", None, "grp"), P("cl", None, "grp")),
        check_vma=False,
    )
```

time: 293 us -> 110 us (0.38)
  blocking collectives: 182 us -> 0 us
  matrix products: 26.5 us -> 0 us
  waiting for transfers between devices: 7.11 us -> 23.7 us
  Pallas kernels: 0 us -> 15.1 us
  other arithmetic: 7.02 us -> 0 us
  starting transfers between devices: 51.9 us -> 55.5 us
  local copies, waits for them, and re-layouts: 17.3 us -> 14.2 us
    all_gather x1 -> x0, blocking collectives: 182 us -> none  [in_one_piece(): out, at, done = (lax.all_gather(both, axis, axis=dim, tiled=True), 0, [])]
    dot_general x17 -> x0, matrix products: 26.5 us -> none  [operator_product(): return jnp.einsum(form, left, right, precision=lax.Precision.HIGHEST)]
    pallas_call x0 -> x9, Pallas kernels: none -> 15.1 us  [the longest x2 3.09 us: shards(): call(near_body, (field, field), [VMEM] * 5, (VMEM, VMEM), 'near')]
    unnamed x24 -> x48, local copies, waits for them, and re-layouts: 2.8 us -> 14.2 us
    gather x4 -> x0, local copies, waits for them, and re-layouts: 10.4 us -> none  [shards(): jnp.take(window, near_index, axis=0) * live_near[:, :, None, None, None]]
    all_to_all x4, waiting for transfers between devices: 7.1 us -> 16.4 us  [exchange(): lax.all_to_all(x, 'cl', split_axis=0, concat_axis=0, tiled=True)]
    ppermute x6, waiting for transfers between devices: 0.02 us -> 7.28 us  [the longest x2 7.27 us: shards(): crossed = lax.ppermute(crossed, 'grp', across)]
    all_to_all x4, starting transfers between devices: 32.2 us -> 37.2 us  [exchange(): lax.all_to_all(x, 'cl', split_axis=0, concat_axis=0, tiled=True)]
  transfers between devices with their start and end apart: 10 -> 10, of which waited for: 3 -> 5; matrix products, arithmetic and copies ran while one was open for 16% -> 0% of each run, Pallas kernels for 0% -> 10%
where the time goes in v1:
time: 110 us; the launch traced here: 109 us
  starting transfers between devices  55.5 us (50%)
  waiting for transfers between devices  23.7 us (22%)
  Pallas kernels  15.1 us (14%)
  local copies, waits for them, and re-layouts  14.2 us (13%)
    all_to_all x4, starting transfers between devices, exchange(): lax.all_to_all(x, 'cl', split_axis=0, concat_axis=0, tiled=True)  37.2 us
    all_to_all x4, waiting for transfers between devices, exchange(): lax.all_to_all(x, 'cl', split_axis=0, concat_axis=0, tiled=True)  16.4 us
    ppermute x2, starting transfers between devices, shards(): after = lax.ppermute(pressure, 'cl', backward)  15.4 us
    unnamed x48, local copies, waits for them, and re-layouts  14.2 us
    ppermute x2, waiting for transfers between devices, shards(): crossed = lax.ppermute(crossed, 'grp', across)  7.27 us
    pallas_call x2, Pallas kernels, shards(): call(near_body, (field, field), [VMEM] * 5, (VMEM, VMEM), 'near')  3.09 us
    pallas_call x1, Pallas kernels, shards(): call(functools.partial(first_transfer_body, rows), (piece, jax.ShapeDtype...  3.03 us
    pallas_call x2, Pallas kernels, shards(): call(functools.partial(update_body, last), (field, field if last else pie...  2.97 us
  transfers between devices with their start and end apart: 10, of which 5 were waited for; matrix products, arithmetic and copies ran while one was open for 0% of the time, Pallas kernels for 10%

profile of v1, /device:TPU:2, one launch (start us, length us, event | category | flops | bytes accessed | tf_op | source)
XLA Modules:
  0.0 109.4 jit_solution(7648957712864002079)
XLA Ops:
  5.1 1.5 %first_moments.1 = f32[512,128]{1,0:T(8,128)} custom-call(f32[2,128,128]{2,1,0:T(8,128)S(1)} %copy-done, f32[2,128,128]{2,1,0:T(8,128)S(1)} %copy-done.4, s32[2,32]{1,0:T(2,128)S(1)} %copy-done.19, s32[2,32]{1,0:T(2,128)S(1)} %copy-done.20, s32[2]{0:T(128)S(1)} %copy-done.22, s32[2]{0:T(128)S(1)} %copy-done.17), custom_call_target="tpu_custom_call" | custom-call | bytes 262144 | tf_op jit(solution)/shard_map/first_moments/pallas_call | solution.py:245
  6.6 13.8 %all-to-all-start = ((f32[64,8,128]{2,1,0:T(8,128)}), f32[64,8,128]{2,1,0:T(8,128)S(1)}, u32[]{:S(2)}, u32[]{:S(2)}) async-start(f32[64,8,128]{2,1,0:T(8,128)} %bitcast), calls=%async_computation | async-start | bytes 524288 | tf_op jit(solution)/shard_map/all_to_all | solution.py:223
  20.4 7.7 %collective-permute-start.1 = (f32[2,128,128]{2,1,0:T(8,128)}, f32[2,128,128]{2,1,0:T(8,128)}, u32[]{:S(2)}, u32[]{:S(2)}) collective-permute-start(f32[2,128,128]{2,1,0:T(8,128)} %incident_ref.3), channel_id=1, source_target_pairs={{1,0},{2,1},{3,2},{4,3},{5,4},{6,5},{7,6},{8,7},{9,8},{10,9},{11,1... | collective-permute-start | bytes 393224 | tf_op jit(solution)/shard_map/ppermute | solution.py:257
  28.1 1.2 %copy-done.6 = f32[16,128,128]{2,1,0:T(8,128)S(1)} copy-done((f32[16,128,128]{2,1,0:T(8,128)S(1)}, f32[16,128,128]{2,1,0:T(8,128)}, u32[]{:S(2)}) %copy-start.6) | copy-done | bytes 1048600
  29.7 6.5 %all-to-all-done = f32[64,8,128]{2,1,0:T(8,128)S(1)} async-done(((f32[64,8,128]{2,1,0:T(8,128)}), f32[64,8,128]{2,1,0:T(8,128)S(1)}, u32[]{:S(2)}, u32[]{:S(2)}) %all-to-all-start) | async-done | bytes 262176 | tf_op jit(solution)/shard_map/all_to_all | solution.py:223
  36.2 3.0 %first_transfer.1 = (f32[256,128]{1,0:T(8,128)}, bf16[16,128,128]{2,1,0:T(8,128)(2,1)S(1)}) custom-call(f32[512,128]{1,0:T(8,128)S(1)} %bitcast.9, bf16[8,256,256]{2,1,0:T(8,128)(2,1)S(1)} %operators.1.ops_ref), custom_call_target="tpu_custom_call" | custom-call | bytes 262144 | tf_op jit(solution)/shard_map/first_transfer/pallas_call | solution.py:265
  39.2 5.5 %all-to-all-start.1 = ((f32[64,4,128]{2,1,0:T(4,128)}), f32[64,4,128]{2,1,0:T(4,128)}, u32[]{:S(2)}, u32[]{:S(2)}) async-start(f32[64,4,128]{2,1,0:T(4,128)} %bitcast.2), calls=%async_computation.1 | async-start | bytes 262144 | tf_op jit(solution)/shard_map/all_to_all | solution.py:223
  44.7 1.6 %copy-done.2 = f32[2,16,128,128]{3,2,1,0:T(8,128)S(1)} copy-done((f32[2,16,128,128]{3,2,1,0:T(8,128)S(1)}, f32[2,16,128,128]{3,2,1,0:T(8,128)}, u32[]{:S(2)}) %copy-start.2) | copy-done | bytes 2097176
  46.3 1.6 %copy-done.3 = f32[2,16,128,128]{3,2,1,0:T(8,128)S(1)} copy-done((f32[2,16,128,128]{3,2,1,0:T(8,128)S(1)}, f32[2,16,128,128]{3,2,1,0:T(8,128)}, u32[]{:S(2)}) %copy-start.3) | copy-done | bytes 2097176
  47.9 1.7 %neighbour_blocks.1 = (bf16[3,512,256]{2,1,0:T(8,128)(2,1)S(1)}, bf16[3,512,256]{2,1,0:T(8,128)(2,1)S(1)}) custom-call(s32[2,16]{1,0:T(2,128)S(1)} %copy-done.21, s32[2]{0:T(128)S(1)} %copy-done.23, f32[1]{0:T(128)} %bitcast.4.sign_ref, f32[2,16,128,128]{3,2,1,0:T(8,128)S(1)} %copy-done.2, f32[2,16,128,128]{3,2,1,0:T(8,128)S(1)} %copy-done.3), custom_call_target="tpu_custom_call" | custom-call | bytes 262144 | tf_op jit(solution)/shard_map/neighbour_blocks/pallas_call | solution.py:229
  49.6 1.5 %near.2 = (f32[2,128,128]{2,1,0:T(8,128)S(1)}, f32[2,128,128]{2,1,0:T(8,128)S(1)}) custom-call(f32[2,128,128]{2,1,0:T(8,128)} %collective-permute-done.before_ref, f32[2,128,128]{2,1,0:T(8,128)S(1)} %copy-done.1, f32[2,128,128]{2,1,0:T(8,128)} %collective-permute-done.1.after_ref, bf16[3,512,256]{2,1,0:T(8,128)(2,1)S(1)} %get-tuple-element.13.top_ref, ...), custom_call_target="tpu_custom_call" | custom-call | bytes 262144 | tf_op jit(solution)/shard_map/near/pallas_call | solution.py:259
  51.8 1.4 %collective-permute-start.2 = (f32[2,128,128]{2,1,0:T(8,128)S(1)}, f32[2,128,128]{2,1,0:T(8,128)S(1)}, u32[]{:S(2)}, u32[]{:S(2)}) collective-permute-start(f32[2,128,128]{2,1,0:T(8,128)S(1)} %get-tuple-element.16), channel_id=1, source_target_pairs={{0,128},{64,192},{128,0},{192,64},{1,129},{65,193},{129,1},{193,65... | collective-permute-start | bytes 393224 | tf_op jit(solution)/shard_map/ppermute | solution.py:262
  53.3 3.5 %collective-permute-done.2.crossed_ref = f32[2,128,128]{2,1,0:T(8,128)S(1)} collective-permute-done((f32[2,128,128]{2,1,0:T(8,128)S(1)}, f32[2,128,128]{2,1,0:T(8,128)S(1)}, u32[]{:S(2)}, u32[]{:S(2)}) %collective-permute-start.2) | collective-permute-done | bytes 131104 | tf_op jit(solution)/shard_map/ppermute | solution.py:262
  59.3 1.5 %update.2 = (f32[2,128,128]{2,1,0:T(8,128)S(1)}, f32[256,128]{1,0:T(8,128)S(1)}) custom-call(f32[256,128]{1,0:T(8,128)} %bitcast.3.in_ref, f32[2,128,128]{2,1,0:T(8,128)S(1)} %copy-done.7, f32[2,128,128]{2,1,0:T(8,128)S(1)} %copy-done.5, s32[2]{0:T(128)S(1)} %copy-done.18, f32[2,128,128]{2,1,0:T(8,128)S(1)} %copy-done.13, f32[2,128,128]{2,1,0:T(8,128)S(1)} %copy-done.15, ...), custom_call_target="tpu_custom_call" | custom-call | bytes 262144 | tf_op jit(solution)/shard_map/update/pallas_call | solution.py:277
  62.1 12.8 %all-to-all-start.2 = ((f32[64,4,128]{2,1,0:T(4,128)}), f32[64,4,128]{2,1,0:T(4,128)S(1)}, u32[]{:S(2)}, u32[]{:S(2)}) async-start(f32[64,4,128]{2,1,0:T(4,128)} %bitcast.12), calls=%async_computation.2 | async-start | bytes 262144 | tf_op jit(solution)/shard_map/all_to_all | solution.py:223
  74.9 7.7 %collective-permute-start.4 = (f32[2,128,128]{2,1,0:T(8,128)}, f32[2,128,128]{2,1,0:T(8,128)}, u32[]{:S(2)}, u32[]{:S(2)}) collective-permute-start(f32[2,128,128]{2,1,0:T(8,128)} %copy-done.9), channel_id=1, source_target_pairs={{1,0},{2,1},{3,2},{4,3},{5,4},{6,5},{7,6},{8,7},{9,8},{10,9},{11,1... | collective-permute-start | bytes 393224 | tf_op jit(solution)/shard_map/ppermute | solution.py:257
  82.5 5.0 %all-to-all-done.2 = f32[64,4,128]{2,1,0:T(4,128)S(1)} async-done(((f32[64,4,128]{2,1,0:T(4,128)}), f32[64,4,128]{2,1,0:T(4,128)S(1)}, u32[]{:S(2)}, u32[]{:S(2)}) %all-to-all-start.2) | async-done | bytes 131104 | tf_op jit(solution)/shard_map/all_to_all | solution.py:223
  87.5 2.5 %next_transfer.1 = f32[256,128]{1,0:T(8,128)} custom-call(f32[256,128]{1,0:T(8,128)S(1)} %bitcast.10, bf16[8,256,256]{2,1,0:T(8,128)(2,1)S(1)} %operators.1.ops_ref, bf16[16,128,128]{2,1,0:T(8,128)(2,1)S(1)} %get-tuple-element.18.counts_ref), custom_call_target="tpu_custom_call" | custom-call | bytes 262144 | tf_op jit(solution)/shard_map/next_transfer/pallas_call | solution.py:273
  90.0 5.2 %all-to-all-start.3 = ((f32[64,4,128]{2,1,0:T(4,128)}), f32[64,4,128]{2,1,0:T(4,128)S(1)}, u32[]{:S(2)}, u32[]{:S(2)}) async-start(f32[64,4,128]{2,1,0:T(4,128)} %bitcast.7), calls=%async_computation.3 | async-start | bytes 262144 | tf_op jit(solution)/shard_map/all_to_all | solution.py:223
  96.2 1.5 %near.3 = (f32[2,128,128]{2,1,0:T(8,128)S(1)}, f32[2,128,128]{2,1,0:T(8,128)S(1)}) custom-call(f32[2,128,128]{2,1,0:T(8,128)} %collective-permute-done.3.before_ref, f32[2,128,128]{2,1,0:T(8,128)S(1)} %copy-done.10, f32[2,128,128]{2,1,0:T(8,128)} %collective-permute-done.4.after_ref, bf16[3,512,256]{2,1,0:T(8,128)(2,1)S(1)} %get-tuple-element.13.top_ref, ...), custom_call_target="tpu_custom_call" | custom-call | bytes 262144 | tf_op jit(solution)/shard_map/near/pallas_call | solution.py:259
  97.7 1.5 %collective-permute-start.5 = (f32[2,128,128]{2,1,0:T(8,128)S(1)}, f32[2,128,128]{2,1,0:T(8,128)S(1)}, u32[]{:S(2)}, u32[]{:S(2)}) collective-permute-start(f32[2,128,128]{2,1,0:T(8,128)S(1)} %get-tuple-element.21), channel_id=1, source_target_pairs={{0,128},{64,192},{128,0},{192,64},{1,129},{65,193},{129,1},{193,65... | collective-permute-start | bytes 393224 | tf_op jit(solution)/shard_map/ppermute | solution.py:262
  99.2 3.7 %collective-permute-done.5.crossed_ref = f32[2,128,128]{2,1,0:T(8,128)S(1)} collective-permute-done((f32[2,128,128]{2,1,0:T(8,128)S(1)}, f32[2,128,128]{2,1,0:T(8,128)S(1)}, u32[]{:S(2)}, u32[]{:S(2)}) %collective-permute-start.5) | collective-permute-done | bytes 131104 | tf_op jit(solution)/shard_map/ppermute | solution.py:262
  102.9 4.9 %all-to-all-done.3 = f32[64,4,128]{2,1,0:T(4,128)S(1)} async-done(((f32[64,4,128]{2,1,0:T(4,128)}), f32[64,4,128]{2,1,0:T(4,128)S(1)}, u32[]{:S(2)}, u32[]{:S(2)}) %all-to-all-start.3) | async-done | bytes 131104 | tf_op jit(solution)/shard_map/all_to_all | solution.py:223
  107.9 1.5 %update.3 = (f32[2,128,128]{2,1,0:T(8,128)}, f32[2,128,128]{2,1,0:T(8,128)}) custom-call(f32[256,128]{1,0:T(8,128)S(1)} %bitcast.11, f32[2,128,128]{2,1,0:T(8,128)S(1)} %copy-done.8, f32[2,128,128]{2,1,0:T(8,128)S(1)} %copy-done.5, s32[2]{0:T(128)S(1)} %copy-done.18, f32[2,128,128]{2,1,0:T(8,128)S(1)} %get-tuple-element.20.straight_ref, ...), custom_call_target="tpu_custom_call" | custom-call | bytes 262144 | tf_op jit(solution)/shard_map/update/pallas_call | solution.py:277
  (53 shorter events, 10.2 us)
Async XLA Ops:
  0.6 0.9 copy-start
  6.6 38.1 %copy-start.21 = (s32[2,16]{1,0:T(2,128)S(1)}, s32[2,16]{1,0:T(2,128)}, u32[]{:S(2)}) copy-start(s32[2,16]{1,0:T(2,128)} %index_ref.1) | copy-start | bytes 388
  6.6 38.1 %copy-start.23 = (s32[2]{0:T(128)S(1)}, s32[2]{0:T(128)}, u32[]{:S(2)}) copy-start(s32[2]{0:T(128)} %count_ref.3) | copy-start | bytes 28
  6.6 29.6 %all-to-all-start = ((f32[64,8,128]{2,1,0:T(8,128)}), f32[64,8,128]{2,1,0:T(8,128)S(1)}, u32[]{:S(2)}, u32[]{:S(2)}) async-start(f32[64,8,128]{2,1,0:T(8,128)} %bitcast), calls=%async_computation | async-start | bytes 524288 | tf_op jit(solution)/shard_map/all_to_all | solution.py:223
  20.4 29.2 %collective-permute-start.1 = (f32[2,128,128]{2,1,0:T(8,128)}, f32[2,128,128]{2,1,0:T(8,128)}, u32[]{:S(2)}, u32[]{:S(2)}) collective-permute-start(f32[2,128,128]{2,1,0:T(8,128)} %incident_ref.3), channel_id=1, source_target_pairs={{1,0},{2,1},{3,2},{4,3},{5,4},{6,5},{7,6},{8,7},{9,8},{10,9},{11,1... | collective-permute-start | bytes 393224 | tf_op jit(solution)/shard_map/ppermute | solution.py:257
  28.1 21.5 %collective-permute-start = (f32[2,128,128]{2,1,0:T(8,128)}, f32[2,128,128]{2,1,0:T(8,128)}, u32[]{:S(2)}, u32[]{:S(2)}) collective-permute-start(f32[2,128,128]{2,1,0:T(8,128)} %incident_ref.3), channel_id=1, source_target_pairs={{0,1},{1,2},{2,3},{3,4},{4,5},{5,6},{6,7},{7,8},{8,9},{9,10},{10,1... | collective-permute-start | bytes 393224 | tf_op jit(solution)/shard_map/ppermute | solution.py:256
  28.1 1.2 %copy-start.6 = (f32[16,128,128]{2,1,0:T(8,128)S(1)}, f32[16,128,128]{2,1,0:T(8,128)}, u32[]{:S(2)}) copy-start(f32[16,128,128]{2,1,0:T(8,128)} %ops_ref.1) | copy-start | bytes 3145732
  39.2 18.2 %all-to-all-start.1 = ((f32[64,4,128]{2,1,0:T(4,128)}), f32[64,4,128]{2,1,0:T(4,128)}, u32[]{:S(2)}, u32[]{:S(2)}) async-start(f32[64,4,128]{2,1,0:T(4,128)} %bitcast.2), calls=%async_computation.1 | async-start | bytes 262144 | tf_op jit(solution)/shard_map/all_to_all | solution.py:223
  44.7 1.6 %copy-start.2 = (f32[2,16,128,128]{3,2,1,0:T(8,128)S(1)}, f32[2,16,128,128]{3,2,1,0:T(8,128)}, u32[]{:S(2)}) copy-start(f32[2,16,128,128]{3,2,1,0:T(8,128)} %real_ref.1) | copy-start | bytes 6291460
  46.3 1.6 %copy-start.3 = (f32[2,16,128,128]{3,2,1,0:T(8,128)S(1)}, f32[2,16,128,128]{3,2,1,0:T(8,128)}, u32[]{:S(2)}) copy-start(f32[2,16,128,128]{3,2,1,0:T(8,128)} %imag_ref.1) | copy-start | bytes 6291460
  47.9 1.7 %copy-start.1 = (f32[2,128,128]{2,1,0:T(8,128)S(1)}, f32[2,128,128]{2,1,0:T(8,128)}, u32[]{:S(2)}) copy-start(f32[2,128,128]{2,1,0:T(8,128)} %incident_ref.3) | copy-start | bytes 393220
  47.9 9.5 %copy-start.5 = (f32[2,128,128]{2,1,0:T(8,128)S(1)}, f32[2,128,128]{2,1,0:T(8,128)}, u32[]{:S(2)}) copy-start(f32[2,128,128]{2,1,0:T(8,128)} %to_moments_ref.5) | copy-start | bytes 393220
  47.9 9.5 %copy-start.7 = (f32[2,128,128]{2,1,0:T(8,128)S(1)}, f32[2,128,128]{2,1,0:T(8,128)}, u32[]{:S(2)}) copy-start(f32[2,128,128]{2,1,0:T(8,128)} %from_locals_ref.3) | copy-start | bytes 393220
  47.9 9.5 %copy-start.18 = (s32[2]{0:T(128)S(1)}, s32[2]{0:T(128)}, u32[]{:S(2)}) copy-start(s32[2]{0:T(128)} %box_ref.5) | copy-start | bytes 28
  51.8 5.0 %collective-permute-start.2 = (f32[2,128,128]{2,1,0:T(8,128)S(1)}, f32[2,128,128]{2,1,0:T(8,128)S(1)}, u32[]{:S(2)}, u32[]{:S(2)}) collective-permute-start(f32[2,128,128]{2,1,0:T(8,128)S(1)} %get-tuple-element.16), channel_id=1, source_target_pairs={{0,128},{64,192},{128,0},{192,64},{1,129},{65,193},{129,1},{193,65... | collective-permute-start | bytes 393224 | tf_op jit(solution)/shard_map/ppermute | solution.py:262
  57.5 0.9 copy-start.13
  62.1 25.4 %all-to-all-start.2 = ((f32[64,4,128]{2,1,0:T(4,128)}), f32[64,4,128]{2,1,0:T(4,128)S(1)}, u32[]{:S(2)}, u32[]{:S(2)}) async-start(f32[64,4,128]{2,1,0:T(4,128)} %bitcast.12), calls=%async_computation.2 | async-start | bytes 262144 | tf_op jit(solution)/shard_map/all_to_all | solution.py:223
  74.9 20.4 %collective-permute-start.4 = (f32[2,128,128]{2,1,0:T(8,128)}, f32[2,128,128]{2,1,0:T(8,128)}, u32[]{:S(2)}, u32[]{:S(2)}) collective-permute-start(f32[2,128,128]{2,1,0:T(8,128)} %copy-done.9), channel_id=1, source_target_pairs={{1,0},{2,1},{3,2},{4,3},{5,4},{6,5},{7,6},{8,7},{9,8},{10,9},{11,1... | collective-permute-start | bytes 393224 | tf_op jit(solution)/shard_map/ppermute | solution.py:257
  82.5 12.7 %collective-permute-start.3 = (f32[2,128,128]{2,1,0:T(8,128)}, f32[2,128,128]{2,1,0:T(8,128)}, u32[]{:S(2)}, u32[]{:S(2)}) collective-permute-start(f32[2,128,128]{2,1,0:T(8,128)} %copy-done.9), channel_id=1, source_target_pairs={{0,1},{1,2},{2,3},{3,4},{4,5},{5,6},{6,7},{7,8},{8,9},{9,10},{10,1... | collective-permute-start | bytes 393224 | tf_op jit(solution)/shard_map/ppermute | solution.py:256
  90.0 17.9 %copy-start.8 = (f32[2,128,128]{2,1,0:T(8,128)S(1)}, f32[2,128,128]{2,1,0:T(8,128)}, u32[]{:S(2)}) copy-start(f32[2,128,128]{2,1,0:T(8,128)} %from_locals_ref.3) | copy-start | bytes 393220
  90.0 17.9 %copy-start.11 = (f32[2,128,128]{2,1,0:T(8,128)S(1)}, f32[2,128,128]{2,1,0:T(8,128)}, u32[]{:S(2)}) copy-start(f32[2,128,128]{2,1,0:T(8,128)} %copy-done.9) | copy-start | bytes 393220
  90.0 17.8 %all-to-all-start.3 = ((f32[64,4,128]{2,1,0:T(4,128)}), f32[64,4,128]{2,1,0:T(4,128)S(1)}, u32[]{:S(2)}, u32[]{:S(2)}) async-start(f32[64,4,128]{2,1,0:T(4,128)} %bitcast.7), calls=%async_computation.3 | async-start | bytes 262144 | tf_op jit(solution)/shard_map/all_to_all | solution.py:223
  95.2 0.9 copy-start.10
  97.7 5.2 %collective-permute-start.5 = (f32[2,128,128]{2,1,0:T(8,128)S(1)}, f32[2,128,128]{2,1,0:T(8,128)S(1)}, u32[]{:S(2)}, u32[]{:S(2)}) collective-permute-start(f32[2,128,128]{2,1,0:T(8,128)S(1)} %get-tuple-element.21), channel_id=1, source_target_pairs={{0,128},{64,192},{128,0},{192,64},{1,129},{65,193},{129,1},{193,65... | collective-permute-start | bytes 393224 | tf_op jit(solution)/shard_map/ppermute | solution.py:262
  (10 other events, 7.1 us)

commit v2 on v1

--- a/solution.py
+++ b/solution.py
@@ -7,8 +7,10 @@
 from jax.experimental.pallas import tpu as pltpu
 from jax.sharding import PartitionSpec as P
 
+
 ITERS = 2
 DAMPING = 0.7
+MIB = (8, 8, 8)
 F32, BF16 = jnp.float32, jnp.bfloat16
 VMEM = pl.BlockSpec(memory_space=pltpu.VMEM)
 SMEM = pl.BlockSpec(memory_space=pltpu.SMEM)
@@ -30,13 +32,12 @@
     return dot(a0, b0, dims) + (dot(a0, b1, dims) + dot(a1, b0, dims))
 
 
-def call(body, outs, in_specs, out_specs, name, mib=16, cycles=0, **more):
+def call(body, outs, in_specs, out_specs, mib=8, cycles=0, **more):
     return pl.pallas_call(
         body,
         out_shape=outs,
         in_specs=in_specs,
         out_specs=out_specs,
-        name=name,
         compiler_params=pltpu.CompilerParams(vmem_limit_bytes=mib << 20),
         cost_estimate=pl.CostEstimate(flops=cycles, bytes_accessed=1 << 18, transcendentals=0),
         **more,
@@ -64,7 +65,8 @@
         out_ref[pl.ds(row, peers, stride=rows), :] = jnp.zeros((peers, lists.shape[1]), F32)
 
 
-def blocks_body(index_ref, count_ref, sign_ref, real_ref, imag_ref, top_ref, rest_ref, total):
+def blocks_body(index_ref, count_ref, place_ref, sign_ref, real_ref, imag_ref, top_ref, rest_ref, total):
+    odd = lax.rem(place_ref[0], 2)
     c, part = pl.program_id(0), pl.program_id(1)
     chunk = real_ref.shape[1]
 
@@ -92,7 +94,8 @@
                         block = block * sign_ref[0]
                     top, rest = halves(block)
                     row = (cluster * 2 + side) * points
-                    here = (j // 2, pl.ds(row, points), pl.ds(j % 2 * points, points))
+                    slot = (2 - 2 * odd, 1, 2 * odd)[j // 2]
+                    here = (slot, pl.ds(row, points), pl.ds(j % 2 * points, points))
                     top_ref[here] = top
                     rest_ref[here] = rest
 
@@ -106,22 +109,21 @@
         out_ref[y // 2, rows, size : 2 * size] = rest
 
 
-def near_body(before_ref, own_ref, after_ref, top_ref, rest_ref, straight_ref, crossed_ref):
+def near_body(first_ref, own_ref, second_ref, top_ref, rest_ref, straight_ref, crossed_ref):
     points = own_ref.shape[1]
     total = None
-    for slab, ref in enumerate((before_ref, own_ref, after_ref)):
+    for slot, ref in enumerate((first_ref, own_ref, second_ref)):
         v0, v1 = halves(jnp.concatenate([ref[0], ref[1]], axis=0))
-        both = dot(top_ref[slab], jnp.concatenate([v0, v1], axis=1))
-        part = both[:, :points] + (both[:, points:] + dot(rest_ref[slab], v0))
+        both = dot(top_ref[slot], jnp.concatenate([v0, v1], axis=1))
+        part = both[:, :points] + (both[:, points:] + dot(rest_ref[slot], v0))
         total = part if total is None else total + part
     for c in range(2):
         straight_ref[c] = total[2 * c * points : (2 * c + 1) * points]
         crossed_ref[c] = total[(2 * c + 1) * points : (2 * c + 2) * points]
 
 
-def interaction_counts(in_ref, rows, counts_ref, kinds):
-    peers = in_ref.shape[0] // rows
-    parts = [in_ref[pl.ds(4 + rows * j, peers // 4, stride=4 * rows), :] for j in range(4)]
+def interaction_counts(lists_ref, first, step, peers, counts_ref):
+    parts = [lists_ref[pl.ds(first + step * j, peers // 4, stride=4 * step), :] for j in range(4)]
     lane = lax.broadcasted_iota(jnp.int32, parts[0].shape, 1)
     low = lane < 64
     turn = [pltpu.roll(p, 64, 1) for p in parts]
@@ -137,7 +139,7 @@
         left = jnp.where(own & ((row >> 3) == kind[i : i + 1, :]), 1.0, 0.0).astype(BF16)
         right = jnp.where(row == source[i : i + 1, :], 1.0, 0.0).astype(BF16)
         block = dot(left, right, NT).astype(BF16)
-        for y in range(kinds):
+        for y in range(counts_ref.shape[0]):
             counts_ref[y, 8 * i : 8 * i + 8, :] = block[8 * y : 8 * y + 8]
 
 
@@ -165,13 +167,16 @@
         out_ref[pl.ds(k, 2 * peers, stride=2), :] = total[k]
 
 
-def first_transfer_body(rows, in_ref, ops_ref, out_ref, counts_ref):
-    interaction_counts(in_ref, rows, counts_ref, counts_ref.shape[0])
+def first_transfer_body(rows, in_ref, ops_ref, out_ref, lists_ref, counts_ref):
+    peers = in_ref.shape[0] // rows
+    lists_ref[...] = in_ref[pl.ds(4, peers, stride=rows), :]
+    interaction_counts(in_ref, 4, rows, peers, counts_ref)
     transfer(in_ref, rows, ops_ref, counts_ref, out_ref)
 
 
-def next_transfer_body(rows, in_ref, ops_ref, counts_ref, out_ref):
-    transfer(in_ref, rows, ops_ref, counts_ref, out_ref)
+def next_transfer_body(in_ref, ops_ref, lists_ref, out_ref, counts_ref):
+    interaction_counts(lists_ref, 0, 1, lists_ref.shape[0], counts_ref)
+    transfer(in_ref, 4, ops_ref, counts_ref, out_ref)
 
 
 def update_body(last, in_ref, from_locals_ref, to_moments_ref, box_ref, straight_ref, crossed_ref, incident_ref, pressure_ref, *outs):
@@ -207,79 +212,80 @@
     far_kind,
     far_count,
 ):
-    clusters, points, width = incident.shape
+    clusters, points, _ = incident.shape
     near_max = near_real.shape[1]
     peers, grp = lax.axis_size("cl"), lax.axis_size("grp")
     kinds, size = transfer_ops.shape[0], transfer_ops.shape[1]
     field = jax.ShapeDtypeStruct(incident.shape, F32)
     rows = 8
-    forward = [(i, (i + 1) % peers) for i in range(peers)]
-    backward = [(target, source) for source, target in forward]
+    first_swap = [(i, i ^ 1) for i in range(peers)]
+    second_swap = [(i, (i + 1 if i % 2 else i - 1) % peers) for i in range(peers)]
     across = [(i, (i + grp // 2) % grp) for i in range(grp)]
     sign = jnp.where(lax.axis_index("grp") < grp // 2, 1.0, -1.0).astype(F32).reshape(1)
+
+    place = lax.axis_index("cl").astype(jnp.int32).reshape(1)
 
     def exchange(x, pieces):
         x = x.reshape(peers, pieces, size)
         return lax.all_to_all(x, "cl", split_axis=0, concat_axis=0, tiled=True).reshape(-1, size)
 
-    chunk = 4
+    chunk = 8
     block = pl.BlockSpec((1, chunk, points, points), lambda c, part: (c, part, 0, 0))
-    halved = jax.ShapeDtypeStruct((3, 4 * points, 2 * points), BF16)
+    halved = jax.ShapeDtypeStruct((3, 2 * clusters * points, 2 * points), BF16)
     whole = pl.BlockSpec(halved.shape, lambda c, part: (0, 0, 0))
-    blocks_top, blocks_rest = call(
+    blocks = call(
         blocks_body,
         (halved, halved),
-        [SMEM, SMEM, SMEM, block, block],
+        [SMEM] * 4 + [block] * 2,
         (whole, whole),
-        "neighbour_blocks",
+        mib=56,
         grid=(clusters, near_max // chunk),
         scratch_shapes=[pltpu.VMEM((6, clusters, 2, points, points), F32)],
-    )(near_index, near_count, sign, near_real, near_imag)
-    operators = call(
-        operators_body,
-        jax.ShapeDtypeStruct((kinds // 2, 2 * size, 2 * size), BF16),
-        [VMEM],
-        VMEM,
-        "operators",
-    )(transfer_ops)
+    )
+    prepare = call(operators_body, jax.ShapeDtypeStruct((kinds // 2, 2 * size, 2 * size), BF16), [VMEM], VMEM)
     sent = call(
         functools.partial(first_moments_body, rows),
         jax.ShapeDtypeStruct((peers * rows, size), F32),
         [VMEM] * 4 + [SMEM] * 2,
         VMEM,
-        "first_moments",
+        mib=56,
     )(incident, to_moments, far_source, far_kind, far_count, cluster_box)
 
     pressure = incident
     for iteration in range(ITERS):
         first, last = iteration == 0, iteration == ITERS - 1
-        before = lax.ppermute(pressure, "cl", forward)
-        after = lax.ppermute(pressure, "cl", backward)
         arrived = exchange(sent, rows if first else 4)
-        straight, crossed = call(near_body, (field, field), [VMEM] * 5, (VMEM, VMEM), "near")(
-            before, pressure, after, blocks_top, blocks_rest
-        )
-        crossed = lax.ppermute(crossed, "grp", across)
+        if first:
+            blocks_top, blocks_rest = blocks(near_index, near_count, place, sign, near_real, near_imag)
+            operators = prepare(transfer_ops)
+        one = lax.ppermute(pressure, "cl", first_swap)
+        two = lax.ppermute(pressure, "cl", second_swap)
         piece = jax.ShapeDtypeStruct((peers * 4, size), F32)
+        scratch = [pltpu.VMEM((kinds, 2 * peers, 2 * peers), BF16)]
         if first:
-            locals_out, counts = call(
+            locals_out, lists = call(
                 functools.partial(first_transfer_body, rows),
-                (piece, jax.ShapeDtypeStruct((kinds, 2 * peers, 2 * peers), BF16)),
+                (piece, jax.ShapeDtypeStruct((peers, size), F32)),
                 [VMEM] * 2,
                 (VMEM, VMEM),
-                "first_transfer",
+                scratch_shapes=scratch,
+                mib=MIB[1],
             )(arrived, operators)
         else:
             locals_out = call(
-                functools.partial(next_transfer_body, 4), piece, [VMEM] * 3, VMEM, "next_transfer"
-            )(arrived, operators, counts)
+                next_transfer_body, piece, [VMEM] * 3, VMEM, scratch_shapes=scratch, mib=MIB[1]
+            )(arrived, operators, lists)
         local = exchange(locals_out, 4)
+        straight, crossed = call(
+            near_body, (field, field), [VMEM] * 5, (VMEM, VMEM), mib=MIB[0]
+        )(one, pressure, two, blocks_top, blocks_rest)
+        crossed = lax.ppermute(crossed, "grp", across)
         pressure, sent = call(
             functools.partial(update_body, last),
             (field, field if last else piece),
             [VMEM] * 3 + [SMEM] + [VMEM] * 4,
             (VMEM, VMEM),
-            "update",
+            mib=MIB[2],
         )(local, from_locals, to_moments, cluster_box, straight, crossed, incident, pressure)
     return (pressure, sent)
 

time: 110 us -> 105 us (0.955)
  local copies, waits for them, and re-layouts: 14.2 us -> 6.49 us
  waiting for transfers between devices: 23.7 us -> 25.5 us
  Pallas kernels: 15.1 us -> 16.8 us
  starting transfers between devices: 55.5 us -> 54.3 us
    unnamed x48 -> x28, local copies, waits for them, and re-layouts: 14.2 us -> 6.49 us
    all_to_all x4, waiting for transfers between devices: 16.4 us -> 18.1 us  [exchange(): lax.all_to_all(x, 'cl', split_axis=0, concat_axis=0, tiled=True)]
    pallas_call x5, Pallas kernels: 7.59 us -> 9.21 us  [the longest x1 4.72 us: shards(): blocks(near_index, near_count, place, sign, near_real, near_imag)]
    all_to_all x4, starting transfers between devices: 37.2 us -> 35.9 us  [exchange(): lax.all_to_all(x, 'cl', split_axis=0, concat_axis=0, tiled=True)]
  transfers between devices with their start and end apart: 10 -> 10, of which waited for: 5 -> 5; matrix products, arithmetic and copies ran while one was open for 0% -> 0% of each run, Pallas kernels for 10% -> 12%
where the time goes in v2:
time: 105 us; the launch traced here: 104 us
  starting transfers between devices  54.3 us (52%)
  waiting for transfers between devices  25.5 us (24%)
  Pallas kernels  16.8 us (16%)
  local copies, waits for them, and re-layouts  6.49 us (6%)
    all_to_all x4, starting transfers between devices, exchange(): lax.all_to_all(x, 'cl', split_axis=0, concat_axis=0, tiled=True)  35.9 us
    all_to_all x4, waiting for transfers between devices, exchange(): lax.all_to_all(x, 'cl', split_axis=0, concat_axis=0, tiled=True)  18.1 us
    ppermute x2, starting transfers between devices, shards(): two = lax.ppermute(pressure, 'cl', second_swap)  15.4 us
    ppermute x2, waiting for transfers between devices, shards(): crossed = lax.ppermute(crossed, 'grp', across)  7.34 us
    unnamed x28, local copies, waits for them, and re-layouts  6.49 us
    pallas_call x1, Pallas kernels, shards(): blocks(near_index, near_count, place, sign, near_real, near_imag)  4.72 us
    ppermute x2, starting transfers between devices, shards(): crossed = lax.ppermute(crossed, 'grp', across)  3.03 us
    pallas_call x1, Pallas kernels, shards(): call(functools.partial(first_transfer_body, rows), (piece, jax.ShapeDtype...  3.02 us
  transfers between devices with their start and end apart: 10, of which 5 were waited for; matrix products, arithmetic and copies ran while one was open for 0% of the time, Pallas kernels for 12%

profile of v2, /device:TPU:2, one launch (start us, length us, event | category | flops | bytes accessed | tf_op | source)
XLA Modules:
  0.0 103.9 jit_solution(4802353181993377460)
XLA Ops:
  0.6 2.0 %shard_map.131 = f32[512,128]{1,0:T(8,128)} custom-call(f32[2,128,128]{2,1,0:T(8,128)} %incident_ref.3, f32[2,128,128]{2,1,0:T(8,128)} %to_moments_ref.5, s32[2,32]{1,0:T(2,128)} %source_ref.1, s32[2,32]{1,0:T(2,128)} %kind_ref.1, s32[2]{0:T(128)} %count_ref.2, s32[2]{0:T(128)} %box_ref.5), custom_call_target="tpu_custom_call" | custom-call | bytes 262144 | tf_op jit(solution)/shard_map/pallas_call | solution.py:246
  2.6 13.7 %all-to-all-start = ((f32[64,8,128]{2,1,0:T(8,128)}), f32[64,8,128]{2,1,0:T(8,128)S(1)}, u32[]{:S(2)}, u32[]{:S(2)}) async-start(f32[64,8,128]{2,1,0:T(8,128)} %bitcast.15), calls=%async_computation | async-start | bytes 524288 | tf_op jit(solution)/shard_map/all_to_all | solution.py:230
  16.3 7.7 %collective-permute-start.1 = (f32[2,128,128]{2,1,0:T(8,128)}, f32[2,128,128]{2,1,0:T(8,128)S(1)}, u32[]{:S(2)}, u32[]{:S(2)}) collective-permute-start(f32[2,128,128]{2,1,0:T(8,128)} %incident_ref.3), channel_id=1, source_target_pairs={{0,63},{1,2},{2,1},{3,4},{4,3},{5,6},{6,5},{7,8},{8,7},{9,10},{10,... | collective-permute-start | bytes 393224 | tf_op jit(solution)/shard_map/ppermute | solution.py:262
  24.0 1.2 %copy-done.6 = f32[16,128,128]{2,1,0:T(8,128)S(1)} copy-done((f32[16,128,128]{2,1,0:T(8,128)S(1)}, f32[16,128,128]{2,1,0:T(8,128)}, u32[]{:S(2)}) %copy-start.6) | copy-done | bytes 1048600
  25.5 6.5 %all-to-all-done = f32[64,8,128]{2,1,0:T(8,128)S(1)} async-done(((f32[64,8,128]{2,1,0:T(8,128)}), f32[64,8,128]{2,1,0:T(8,128)S(1)}, u32[]{:S(2)}, u32[]{:S(2)}) %all-to-all-start) | async-done | bytes 262176 | tf_op jit(solution)/shard_map/all_to_all | solution.py:230
  32.0 3.0 %shard_map.133 = (f32[256,128]{1,0:T(8,128)}, f32[64,128]{1,0:T(8,128)S(1)}) custom-call(f32[512,128]{1,0:T(8,128)S(1)} %bitcast.10, bf16[8,256,256]{2,1,0:T(8,128)(2,1)S(1)} %shard_map.132.ops_ref), custom_call_target="tpu_custom_call" | custom-call | bytes 262144 | tf_op jit(solution)/shard_map/pallas_call | solution.py:266
  35.1 4.6 %all-to-all-start.1 = ((f32[64,4,128]{2,1,0:T(4,128)}), f32[64,4,128]{2,1,0:T(4,128)S(1)}, u32[]{:S(2)}, u32[]{:S(2)}) async-start(f32[64,4,128]{2,1,0:T(4,128)} %bitcast.2), calls=%async_computation.1 | async-start | bytes 262144 | tf_op jit(solution)/shard_map/all_to_all | solution.py:230
  39.8 4.7 %shard_map.134 = (bf16[3,512,256]{2,1,0:T(8,128)(2,1)}, bf16[3,512,256]{2,1,0:T(8,128)(2,1)}) custom-call(s32[2,16]{1,0:T(2,128)} %index_ref.1, s32[2]{0:T(128)} %count_ref.3, s32[1]{0:T(128)} %bitcast.4.place_ref, f32[1]{0:T(128)} %bitcast.5.sign_ref, f32[2,16,128,128]{3,2,1,0:T(8,128)} %real_ref.1, f32[2,16,128,128]{3,2,1,0:T(8,128)} %imag_ref.1), custom_call_target="tpu_custom_call" | custom-call | bytes 262144 | tf_op jit(solution)/shard_map/pallas_call | solution.py:259
  45.2 1.1 %copy-done.1 = bf16[3,512,256]{2,1,0:T(8,128)(2,1)S(1)} copy-done((bf16[3,512,256]{2,1,0:T(8,128)(2,1)S(1)}, bf16[3,512,256]{2,1,0:T(8,128)(2,1)}, u32[]{:S(2)}) %copy-start.1) | copy-done | bytes 786456
  46.3 1.1 %copy-done.3 = bf16[3,512,256]{2,1,0:T(8,128)(2,1)S(1)} copy-done((bf16[3,512,256]{2,1,0:T(8,128)(2,1)S(1)}, bf16[3,512,256]{2,1,0:T(8,128)(2,1)}, u32[]{:S(2)}) %copy-start.3) | copy-done | bytes 786456
  47.4 0.9 copy-done.10
  48.9 1.5 %collective-permute-start.2 = (f32[2,128,128]{2,1,0:T(8,128)S(1)}, f32[2,128,128]{2,1,0:T(8,128)S(1)}, u32[]{:S(2)}, u32[]{:S(2)}) collective-permute-start(f32[2,128,128]{2,1,0:T(8,128)S(1)} %get-tuple-element.16), channel_id=1, source_target_pairs={{0,128},{64,192},{128,0},{192,64},{1,129},{65,193},{129,1},{193,65... | collective-permute-start | bytes 393224 | tf_op jit(solution)/shard_map/ppermute | solution.py:282
  50.4 3.5 %collective-permute-done.2.crossed_ref = f32[2,128,128]{2,1,0:T(8,128)S(1)} collective-permute-done((f32[2,128,128]{2,1,0:T(8,128)S(1)}, f32[2,128,128]{2,1,0:T(8,128)S(1)}, u32[]{:S(2)}, u32[]{:S(2)}) %collective-permute-start.2) | collective-permute-done | bytes 131104 | tf_op jit(solution)/shard_map/ppermute | solution.py:282
  54.0 1.1 %shard_map.136 = (f32[2,128,128]{2,1,0:T(8,128)S(1)}, f32[256,128]{1,0:T(8,128)S(1)}) custom-call(f32[256,128]{1,0:T(8,128)S(1)} %bitcast.11, f32[2,128,128]{2,1,0:T(8,128)S(1)} %copy-done.7, f32[2,128,128]{2,1,0:T(8,128)S(1)} %copy-done.5, s32[2]{0:T(128)S(1)} %copy-done.13, f32[2,128,128]{2,1,0:T(8,128)S(1)} %get-tuple-element.15.straight_ref, ...), custom_call_target="tpu_custom_call" | custom-call | bytes 262144 | tf_op jit(solution)/shard_map/pallas_call | solution.py:283
  55.8 12.9 %all-to-all-start.2 = ((f32[64,4,128]{2,1,0:T(4,128)}), f32[64,4,128]{2,1,0:T(4,128)S(1)}, u32[]{:S(2)}, u32[]{:S(2)}) async-start(f32[64,4,128]{2,1,0:T(4,128)} %bitcast.14), calls=%async_computation.2 | async-start | bytes 262144 | tf_op jit(solution)/shard_map/all_to_all | solution.py:230
  68.6 7.7 %collective-permute-start.4 = (f32[2,128,128]{2,1,0:T(8,128)S(1)}, f32[2,128,128]{2,1,0:T(8,128)S(1)}, u32[]{:S(2)}, u32[]{:S(2)}) collective-permute-start(f32[2,128,128]{2,1,0:T(8,128)S(1)} %get-tuple-element.19.own_ref.pressure_ref), channel_id=1, source_target_pairs={{0,63},{1,2},{2,1},{3,4},{4,3},{5,6},{6,5},{7,8},{8,7},{9,10},{10,... | collective-permute-start | bytes 393224 | tf_op jit(solution)/shard_map/ppermute | solution.py:262
  76.3 4.9 %all-to-all-done.2 = f32[64,4,128]{2,1,0:T(4,128)S(1)} async-done(((f32[64,4,128]{2,1,0:T(4,128)}), f32[64,4,128]{2,1,0:T(4,128)S(1)}, u32[]{:S(2)}, u32[]{:S(2)}) %all-to-all-start.2) | async-done | bytes 131104 | tf_op jit(solution)/shard_map/all_to_all | solution.py:230
  81.3 0.8 copy-done.12
  82.0 3.0 %shard_map.137 = f32[256,128]{1,0:T(8,128)} custom-call(f32[256,128]{1,0:T(8,128)S(1)} %bitcast.13, bf16[8,256,256]{2,1,0:T(8,128)(2,1)S(1)} %shard_map.132.ops_ref, f32[64,128]{1,0:T(8,128)S(1)} %copy-done.12), custom_call_target="tpu_custom_call" | custom-call | bytes 262144 | tf_op jit(solution)/shard_map/pallas_call | solution.py:275
  85.0 4.7 %all-to-all-start.3 = ((f32[64,4,128]{2,1,0:T(4,128)}), f32[64,4,128]{2,1,0:T(4,128)S(1)}, u32[]{:S(2)}, u32[]{:S(2)}) async-start(f32[64,4,128]{2,1,0:T(4,128)} %bitcast.8), calls=%async_computation.3 | async-start | bytes 262144 | tf_op jit(solution)/shard_map/all_to_all | solution.py:230
  90.3 1.5 %collective-permute-start.5 = (f32[2,128,128]{2,1,0:T(8,128)S(1)}, f32[2,128,128]{2,1,0:T(8,128)S(1)}, u32[]{:S(2)}, u32[]{:S(2)}) collective-permute-start(f32[2,128,128]{2,1,0:T(8,128)S(1)} %get-tuple-element.21), channel_id=1, source_target_pairs={{0,128},{64,192},{128,0},{192,64},{1,129},{65,193},{129,1},{193,65... | collective-permute-start | bytes 393224 | tf_op jit(solution)/shard_map/ppermute | solution.py:282
  91.9 3.8 %collective-permute-done.5.crossed_ref = f32[2,128,128]{2,1,0:T(8,128)S(1)} collective-permute-done((f32[2,128,128]{2,1,0:T(8,128)S(1)}, f32[2,128,128]{2,1,0:T(8,128)S(1)}, u32[]{:S(2)}, u32[]{:S(2)}) %collective-permute-start.5) | collective-permute-done | bytes 131104 | tf_op jit(solution)/shard_map/ppermute | solution.py:282
  95.7 6.7 %all-to-all-done.3 = f32[64,4,128]{2,1,0:T(4,128)S(1)} async-done(((f32[64,4,128]{2,1,0:T(4,128)}), f32[64,4,128]{2,1,0:T(4,128)S(1)}, u32[]{:S(2)}, u32[]{:S(2)}) %all-to-all-start.3) | async-done | bytes 131104 | tf_op jit(solution)/shard_map/all_to_all | solution.py:230
  102.4 1.5 %shard_map.139 = (f32[2,128,128]{2,1,0:T(8,128)}, f32[2,128,128]{2,1,0:T(8,128)}) custom-call(f32[256,128]{1,0:T(8,128)S(1)} %bitcast.12, f32[2,128,128]{2,1,0:T(8,128)S(1)} %copy-done.7, f32[2,128,128]{2,1,0:T(8,128)S(1)} %copy-done.5, s32[2]{0:T(128)S(1)} %copy-done.13, f32[2,128,128]{2,1,0:T(8,128)S(1)} %get-tuple-element.20.straight_ref, ...), custom_call_target="tpu_custom_call" | custom-call | bytes 262144 | tf_op jit(solution)/shard_map/pallas_call | solution.py:283
  (33 shorter events, 2.9 us)
Async XLA Ops:
  2.6 29.4 %all-to-all-start = ((f32[64,8,128]{2,1,0:T(8,128)}), f32[64,8,128]{2,1,0:T(8,128)S(1)}, u32[]{:S(2)}, u32[]{:S(2)}) async-start(f32[64,8,128]{2,1,0:T(8,128)} %bitcast.15), calls=%async_computation | async-start | bytes 524288 | tf_op jit(solution)/shard_map/all_to_all | solution.py:230
  16.3 28.2 %collective-permute-start.1 = (f32[2,128,128]{2,1,0:T(8,128)}, f32[2,128,128]{2,1,0:T(8,128)S(1)}, u32[]{:S(2)}, u32[]{:S(2)}) collective-permute-start(f32[2,128,128]{2,1,0:T(8,128)} %incident_ref.3), channel_id=1, source_target_pairs={{0,63},{1,2},{2,1},{3,4},{4,3},{5,6},{6,5},{7,8},{8,7},{9,10},{10,... | collective-permute-start | bytes 393224 | tf_op jit(solution)/shard_map/ppermute | solution.py:262
  24.0 20.5 %collective-permute-start = (f32[2,128,128]{2,1,0:T(8,128)}, f32[2,128,128]{2,1,0:T(8,128)S(1)}, u32[]{:S(2)}, u32[]{:S(2)}) collective-permute-start(f32[2,128,128]{2,1,0:T(8,128)} %incident_ref.3), channel_id=1, source_target_pairs={{0,1},{1,0},{2,3},{3,2},{4,5},{5,4},{6,7},{7,6},{8,9},{9,8},{10,11... | collective-permute-start | bytes 393224 | tf_op jit(solution)/shard_map/ppermute | solution.py:261
  24.0 1.2 %copy-start.6 = (f32[16,128,128]{2,1,0:T(8,128)S(1)}, f32[16,128,128]{2,1,0:T(8,128)}, u32[]{:S(2)}) copy-start(f32[16,128,128]{2,1,0:T(8,128)} %ops_ref.1) | copy-start | bytes 3145732
  35.1 4.7 %copy-start.11 = (f32[64,128]{1,0:T(8,128)}, f32[64,128]{1,0:T(8,128)S(1)}, u32[]{:S(2)}) copy-start(f32[64,128]{1,0:T(8,128)S(1)} %get-tuple-element.18.lists_ref) | copy-start | bytes 98308
  35.1 18.9 %all-to-all-start.1 = ((f32[64,4,128]{2,1,0:T(4,128)}), f32[64,4,128]{2,1,0:T(4,128)S(1)}, u32[]{:S(2)}, u32[]{:S(2)}) async-start(f32[64,4,128]{2,1,0:T(4,128)} %bitcast.2), calls=%async_computation.1 | async-start | bytes 262144 | tf_op jit(solution)/shard_map/all_to_all | solution.py:230
  39.7 5.4 %copy-start = (f32[2,128,128]{2,1,0:T(8,128)S(1)}, f32[2,128,128]{2,1,0:T(8,128)}, u32[]{:S(2)}) copy-start(f32[2,128,128]{2,1,0:T(8,128)} %incident_ref.3) | copy-start | bytes 393220
  39.7 14.2 %copy-start.5 = (f32[2,128,128]{2,1,0:T(8,128)S(1)}, f32[2,128,128]{2,1,0:T(8,128)}, u32[]{:S(2)}) copy-start(f32[2,128,128]{2,1,0:T(8,128)} %to_moments_ref.5) | copy-start | bytes 393220
  39.8 14.2 %copy-start.7 = (f32[2,128,128]{2,1,0:T(8,128)S(1)}, f32[2,128,128]{2,1,0:T(8,128)}, u32[]{:S(2)}) copy-start(f32[2,128,128]{2,1,0:T(8,128)} %from_locals_ref.3) | copy-start | bytes 393220
  39.8 14.2 %copy-start.13 = (s32[2]{0:T(128)S(1)}, s32[2]{0:T(128)}, u32[]{:S(2)}) copy-start(s32[2]{0:T(128)} %box_ref.5) | copy-start | bytes 28
  44.5 0.7 copy-start.9
  45.2 1.1 %copy-start.1 = (bf16[3,512,256]{2,1,0:T(8,128)(2,1)S(1)}, bf16[3,512,256]{2,1,0:T(8,128)(2,1)}, u32[]{:S(2)}) copy-start(bf16[3,512,256]{2,1,0:T(8,128)(2,1)} %get-tuple-element.13.top_ref) | copy-start | bytes 2359300
  46.3 1.1 %copy-start.3 = (bf16[3,512,256]{2,1,0:T(8,128)(2,1)S(1)}, bf16[3,512,256]{2,1,0:T(8,128)(2,1)}, u32[]{:S(2)}) copy-start(bf16[3,512,256]{2,1,0:T(8,128)(2,1)} %get-tuple-element.14.rest_ref) | copy-start | bytes 2359300
  47.4 0.9 copy-start.10
  48.3 41.4 %copy-start.2 = (bf16[3,512,256]{2,1,0:T(8,128)(2,1)S(1)}, bf16[3,512,256]{2,1,0:T(8,128)(2,1)}, u32[]{:S(2)}) copy-start(bf16[3,512,256]{2,1,0:T(8,128)(2,1)} %get-tuple-element.13.top_ref) | copy-start | bytes 2359300
  48.3 41.4 %copy-start.4 = (bf16[3,512,256]{2,1,0:T(8,128)(2,1)S(1)}, bf16[3,512,256]{2,1,0:T(8,128)(2,1)}, u32[]{:S(2)}) copy-start(bf16[3,512,256]{2,1,0:T(8,128)(2,1)} %get-tuple-element.14.rest_ref) | copy-start | bytes 2359300
  48.9 5.1 %collective-permute-start.2 = (f32[2,128,128]{2,1,0:T(8,128)S(1)}, f32[2,128,128]{2,1,0:T(8,128)S(1)}, u32[]{:S(2)}, u32[]{:S(2)}) collective-permute-start(f32[2,128,128]{2,1,0:T(8,128)S(1)} %get-tuple-element.16), channel_id=1, source_target_pairs={{0,128},{64,192},{128,0},{192,64},{1,129},{65,193},{129,1},{193,65... | collective-permute-start | bytes 393224 | tf_op jit(solution)/shard_map/ppermute | solution.py:282
  55.1 0.7 copy-start.8
  55.8 25.5 %all-to-all-start.2 = ((f32[64,4,128]{2,1,0:T(4,128)}), f32[64,4,128]{2,1,0:T(4,128)S(1)}, u32[]{:S(2)}, u32[]{:S(2)}) async-start(f32[64,4,128]{2,1,0:T(4,128)} %bitcast.14), calls=%async_computation.2 | async-start | bytes 262144 | tf_op jit(solution)/shard_map/all_to_all | solution.py:230
  68.6 21.1 %collective-permute-start.4 = (f32[2,128,128]{2,1,0:T(8,128)S(1)}, f32[2,128,128]{2,1,0:T(8,128)S(1)}, u32[]{:S(2)}, u32[]{:S(2)}) collective-permute-start(f32[2,128,128]{2,1,0:T(8,128)S(1)} %get-tuple-element.19.own_ref.pressure_ref), channel_id=1, source_target_pairs={{0,63},{1,2},{2,1},{3,4},{4,3},{5,6},{6,5},{7,8},{8,7},{9,10},{10,... | collective-permute-start | bytes 393224 | tf_op jit(solution)/shard_map/ppermute | solution.py:262
  76.3 13.4 %collective-permute-start.3 = (f32[2,128,128]{2,1,0:T(8,128)S(1)}, f32[2,128,128]{2,1,0:T(8,128)S(1)}, u32[]{:S(2)}, u32[]{:S(2)}) collective-permute-start(f32[2,128,128]{2,1,0:T(8,128)S(1)} %get-tuple-element.19.own_ref.pressure_ref), channel_id=1, source_target_pairs={{0,1},{1,0},{2,3},{3,2},{4,5},{5,4},{6,7},{7,6},{8,9},{9,8},{10,11... | collective-permute-start | bytes 393224 | tf_op jit(solution)/shard_map/ppermute | solution.py:261
  81.3 0.8 copy-start.12
  85.0 17.4 %all-to-all-start.3 = ((f32[64,4,128]{2,1,0:T(4,128)}), f32[64,4,128]{2,1,0:T(4,128)S(1)}, u32[]{:S(2)}, u32[]{:S(2)}) async-start(f32[64,4,128]{2,1,0:T(4,128)} %bitcast.8), calls=%async_computation.3 | async-start | bytes 262144 | tf_op jit(solution)/shard_map/all_to_all | solution.py:230
  90.3 5.3 %collective-permute-start.5 = (f32[2,128,128]{2,1,0:T(8,128)S(1)}, f32[2,128,128]{2,1,0:T(8,128)S(1)}, u32[]{:S(2)}, u32[]{:S(2)}) collective-permute-start(f32[2,128,128]{2,1,0:T(8,128)S(1)} %get-tuple-element.21), channel_id=1, source_target_pairs={{0,128},{64,192},{128,0},{192,64},{1,129},{65,193},{129,1},{193,65... | collective-permute-start | bytes 393224 | tf_op jit(solution)/shard_map/ppermute | solution.py:282

commit v3 on v2

--- a/solution.py
+++ b/solution.py
@@ -109,7 +109,9 @@
         out_ref[y // 2, rows, size : 2 * size] = rest
 
 
-def near_body(first_ref, own_ref, second_ref, top_ref, rest_ref, straight_ref, crossed_ref):
+def near_body(first, first_ref, own_ref, second_ref, top_ref, rest_ref, *rest):
+    incident_ref = own_ref if first else rest[0]
+    base_ref, crossed_ref = rest[-2:]
     points = own_ref.shape[1]
     total = None
     for slot, ref in enumerate((first_ref, own_ref, second_ref)):
@@ -118,12 +120,13 @@
         part = both[:, :points] + (both[:, points:] + dot(rest_ref[slot], v0))
         total = part if total is None else total + part
     for c in range(2):
-        straight_ref[c] = total[2 * c * points : (2 * c + 1) * points]
+        base_ref[c] = (incident_ref[c] - own_ref[c]) - total[2 * c * points : (2 * c + 1) * points]
         crossed_ref[c] = total[(2 * c + 1) * points : (2 * c + 2) * points]
 
 
-def interaction_counts(lists_ref, first, step, peers, counts_ref):
-    parts = [lists_ref[pl.ds(first + step * j, peers // 4, stride=4 * step), :] for j in range(4)]
+def interaction_counts(in_ref, at, rows, counts_ref):
+    peers = in_ref.shape[0] // rows
+    parts = [in_ref[pl.ds(at + rows * j, peers // 4, stride=4 * rows), :] for j in range(4)]
     lane = lax.broadcasted_iota(jnp.int32, parts[0].shape, 1)
     low = lane < 64
     turn = [pltpu.roll(p, 64, 1) for p in parts]
@@ -143,7 +146,7 @@
             counts_ref[y, 8 * i : 8 * i + 8, :] = block[8 * y : 8 * y + 8]
 
 
-def transfer(in_ref, rows, ops_ref, counts_ref, out_ref):
+def transfer(in_ref, ops_ref, counts_ref, out_ref, rows):
     peers, size = in_ref.shape[0] // rows, in_ref.shape[1]
     moments = []
     for k in range(2):
@@ -168,18 +171,17 @@
 
 
 def first_transfer_body(rows, in_ref, ops_ref, out_ref, lists_ref, counts_ref):
-    peers = in_ref.shape[0] // rows
-    lists_ref[...] = in_ref[pl.ds(4, peers, stride=rows), :]
-    interaction_counts(in_ref, 4, rows, peers, counts_ref)
-    transfer(in_ref, rows, ops_ref, counts_ref, out_ref)
+    lists_ref[...] = in_ref[pl.ds(4, lists_ref.shape[0], stride=rows), :]
+    interaction_counts(in_ref, 4, rows, counts_ref)
+    transfer(in_ref, ops_ref, counts_ref, out_ref, rows)
 
 
 def next_transfer_body(in_ref, ops_ref, lists_ref, out_ref, counts_ref):
-    interaction_counts(lists_ref, 0, 1, lists_ref.shape[0], counts_ref)
-    transfer(in_ref, 4, ops_ref, counts_ref, out_ref)
-
-
-def update_body(last, in_ref, from_locals_ref, to_moments_ref, box_ref, straight_ref, crossed_ref, incident_ref, pressure_ref, *outs):
+    interaction_counts(lists_ref, 0, 1, counts_ref)
+    transfer(in_ref, ops_ref, counts_ref, out_ref, 4)
+
+
+def update_body(last, in_ref, from_locals_ref, to_moments_ref, box_ref, base_ref, crossed_ref, pressure_ref, *outs):
     peers = in_ref.shape[0] // 4
     local = []
     for b in range(2):
@@ -187,8 +189,7 @@
     fields = []
     for c in range(2):
         far = product(from_locals_ref[c], jnp.where(box_ref[c] == 0, local[0], local[1]), NT)
-        applied = pressure_ref[c] + (straight_ref[c] + crossed_ref[c]) + far
-        residual = incident_ref[c] - applied
+        residual = base_ref[c] - (crossed_ref[c] + far)
         field = pressure_ref[c] + DAMPING * residual
         fields.append(field)
         outs[0][c] = field
@@ -217,7 +218,7 @@
     peers, grp = lax.axis_size("cl"), lax.axis_size("grp")
     kinds, size = transfer_ops.shape[0], transfer_ops.shape[1]
     field = jax.ShapeDtypeStruct(incident.shape, F32)
-    rows = 8
+    rows = 5
     first_swap = [(i, i ^ 1) for i in range(peers)]
     second_swap = [(i, (i + 1 if i % 2 else i - 1) % peers) for i in range(peers)]
     across = [(i, (i + grp // 2) % grp) for i in range(grp)]
@@ -226,7 +227,7 @@
     place = lax.axis_index("cl").astype(jnp.int32).reshape(1)
 
     def exchange(x, pieces):
-        x = x.reshape(peers, pieces, size)
+        x = x.reshape((peers, pieces, size) if pieces == 4 else (peers, pieces, 1, size))
         return lax.all_to_all(x, "cl", split_axis=0, concat_axis=0, tiled=True).reshape(-1, size)
 
     chunk = 8
@@ -261,32 +262,27 @@
         one = lax.ppermute(pressure, "cl", first_swap)
         two = lax.ppermute(pressure, "cl", second_swap)
         piece = jax.ShapeDtypeStruct((peers * 4, size), F32)
-        scratch = [pltpu.VMEM((kinds, 2 * peers, 2 * peers), BF16)]
+        shared = dict(mib=MIB[1], scratch_shapes=[pltpu.VMEM((kinds, 2 * peers, 2 * peers), BF16)])
         if first:
+            outs = (piece, jax.ShapeDtypeStruct((peers, size), F32))
             locals_out, lists = call(
-                functools.partial(first_transfer_body, rows),
-                (piece, jax.ShapeDtypeStruct((peers, size), F32)),
-                [VMEM] * 2,
-                (VMEM, VMEM),
-                scratch_shapes=scratch,
-                mib=MIB[1],
+                functools.partial(first_transfer_body, rows), outs, [VMEM] * 2, (VMEM, VMEM), **shared
             )(arrived, operators)
         else:
-            locals_out = call(
-                next_transfer_body, piece, [VMEM] * 3, VMEM, scratch_shapes=scratch, mib=MIB[1]
-            )(arrived, operators, lists)
+            locals_out = call(next_transfer_body, piece, [VMEM] * 3, VMEM, **shared)(arrived, operators, lists)
         local = exchange(locals_out, 4)
-        straight, crossed = call(
-            near_body, (field, field), [VMEM] * 5, (VMEM, VMEM), mib=MIB[0]
-        )(one, pressure, two, blocks_top, blocks_rest)
+        more = () if first else (incident,)
+        base, crossed = call(
+            functools.partial(near_body, first), (field, field), [VMEM] * (5 + len(more)), (VMEM, VMEM), mib=MIB[0]
+        )(one, pressure, two, blocks_top, blocks_rest, *more)
         crossed = lax.ppermute(crossed, "grp", across)
         pressure, sent = call(
             functools.partial(update_body, last),
             (field, field if last else piece),
-            [VMEM] * 3 + [SMEM] + [VMEM] * 4,
+            [VMEM] * 3 + [SMEM] + [VMEM] * 3,
             (VMEM, VMEM),
             mib=MIB[2],
-        )(local, from_locals, to_moments, cluster_box, straight, crossed, incident, pressure)
+        )(local, from_locals, to_moments, cluster_box, base, crossed, pressure)
     return (pressure, sent)
 
 

time: 105 us -> 102 us (0.971)
  waiting for transfers between devices: 25.5 us -> 23.9 us
  local copies, waits for them, and re-layouts: 6.49 us -> 4.89 us
    all_to_all x4, waiting for transfers between devices: 18.1 us -> 16.5 us  [exchange(): lax.all_to_all(x, 'cl', split_axis=0, concat_axis=0, tiled=True)]
    unnamed x28 -> x22, local copies, waits for them, and re-layouts: 6.49 us -> 4.89 us
where the time goes in v3:
time: 102 us; the launch traced here: 101 us
  starting transfers between devices  54.2 us (53%)
  waiting for transfers between devices  23.9 us (23%)
  Pallas kernels  17.4 us (17%)
  local copies, waits for them, and re-layouts  4.89 us (5%)
    all_to_all x4, starting transfers between devices, exchange(): lax.all_to_all(x, 'cl', split_axis=0, concat_axis=0, tiled=True)  35.8 us
    all_to_all x4, waiting for transfers between devices, exchange(): lax.all_to_all(x, 'cl', split_axis=0, concat_axis=0, tiled=True)  16.5 us
    ppermute x2, starting transfers between devices, shards(): two = lax.ppermute(pressure, 'cl', second_swap)  15.4 us
    ppermute x2, waiting for transfers between devices, shards(): crossed = lax.ppermute(crossed, 'grp', across)  7.36 us
    unnamed x22, local copies, waits for them, and re-layouts  4.89 us
    pallas_call x1, Pallas kernels, shards(): blocks(near_index, near_count, place, sign, near_real, near_imag)  4.72 us
    pallas_call x2, Pallas kernels, shards(): call(functools.partial(update_body, last), (field, field if last else pie...  3.26 us
    ppermute x2, starting transfers between devices, shards(): crossed = lax.ppermute(crossed, 'grp', across)  3.02 us
  transfers between devices with their start and end apart: 10, of which 5 were waited for; matrix products, arithmetic and copies ran while one was open for 0% of the time, Pallas kernels for 12%

profile of v3, /device:TPU:2, one launch (start us, length us, event | category | flops | bytes accessed | tf_op | source)
XLA Modules:
  0.0 101.1 jit_solution(4940729342906266161)
XLA Ops:
  0.6 1.9 %shard_map.131 = f32[320,128]{1,0:T(8,128)} custom-call(f32[2,128,128]{2,1,0:T(8,128)} %rest_0_.1, f32[2,128,128]{2,1,0:T(8,128)} %to_moments_ref.5, s32[2,32]{1,0:T(2,128)} %source_ref.1, s32[2,32]{1,0:T(2,128)} %kind_ref.1, s32[2]{0:T(128)} %count_ref.2, s32[2]{0:T(128)} %box_ref.5), custom_call_target="tpu_custom_call" | custom-call | bytes 262144 | tf_op jit(solution)/shard_map/pallas_call | solution.py:247
  2.6 13.7 %all-to-all-start = ((f32[64,5,1,128]{3,2,1,0:T(1,128)}), f32[64,5,1,128]{3,2,1,0:T(1,128)S(1)}, u32[]{:S(2)}, u32[]{:S(2)}) async-start(f32[64,5,1,128]{3,2,1,0:T(1,128)} %bitcast.14), calls=%async_computation | async-start | bytes 327680 | tf_op jit(solution)/shard_map/all_to_all | solution.py:231
  16.2 7.7 %collective-permute-start.1 = (f32[2,128,128]{2,1,0:T(8,128)}, f32[2,128,128]{2,1,0:T(8,128)S(1)}, u32[]{:S(2)}, u32[]{:S(2)}) collective-permute-start(f32[2,128,128]{2,1,0:T(8,128)} %rest_0_.1), channel_id=1, source_target_pairs={{0,63},{1,2},{2,1},{3,4},{4,3},{5,6},{6,5},{7,8},{8,7},{9,10},{10,... | collective-permute-start | bytes 393224 | tf_op jit(solution)/shard_map/ppermute | solution.py:263
  23.9 1.2 %copy-done.6 = f32[16,128,128]{2,1,0:T(8,128)S(1)} copy-done((f32[16,128,128]{2,1,0:T(8,128)S(1)}, f32[16,128,128]{2,1,0:T(8,128)}, u32[]{:S(2)}) %copy-start.6) | copy-done | bytes 1048600
  25.5 4.9 %all-to-all-done = f32[64,5,1,128]{3,2,1,0:T(1,128)S(1)} async-done(((f32[64,5,1,128]{3,2,1,0:T(1,128)}), f32[64,5,1,128]{3,2,1,0:T(1,128)S(1)}, u32[]{:S(2)}, u32[]{:S(2)}) %all-to-all-start) | async-done | bytes 163872 | tf_op jit(solution)/shard_map/all_to_all | solution.py:231
  30.4 3.0 %shard_map.133 = (f32[256,128]{1,0:T(8,128)}, f32[64,128]{1,0:T(8,128)S(1)}) custom-call(f32[320,128]{1,0:T(8,128)S(1)} %bitcast.10, bf16[8,256,256]{2,1,0:T(8,128)(2,1)S(1)} %shard_map.132.ops_ref), custom_call_target="tpu_custom_call" | custom-call | bytes 262144 | tf_op jit(solution)/shard_map/pallas_call | solution.py:268
  33.4 0.6 copy-done.8
  34.0 4.6 %all-to-all-start.1 = ((f32[64,4,128]{2,1,0:T(4,128)}), f32[64,4,128]{2,1,0:T(4,128)S(1)}, u32[]{:S(2)}, u32[]{:S(2)}) async-start(f32[64,4,128]{2,1,0:T(4,128)} %bitcast.2), calls=%async_computation.1 | async-start | bytes 262144 | tf_op jit(solution)/shard_map/all_to_all | solution.py:231
  38.7 4.7 %shard_map.134 = (bf16[3,512,256]{2,1,0:T(8,128)(2,1)}, bf16[3,512,256]{2,1,0:T(8,128)(2,1)}) custom-call(s32[2,16]{1,0:T(2,128)} %index_ref.1, s32[2]{0:T(128)} %count_ref.3, s32[1]{0:T(128)} %bitcast.4.place_ref, f32[1]{0:T(128)} %bitcast.5.sign_ref, f32[2,16,128,128]{3,2,1,0:T(8,128)} %real_ref.1, f32[2,16,128,128]{3,2,1,0:T(8,128)} %imag_ref.1), custom_call_target="tpu_custom_call" | custom-call | bytes 262144 | tf_op jit(solution)/shard_map/pallas_call | solution.py:260
  43.4 1.1 %copy-done = bf16[3,512,256]{2,1,0:T(8,128)(2,1)S(1)} copy-done((bf16[3,512,256]{2,1,0:T(8,128)(2,1)S(1)}, bf16[3,512,256]{2,1,0:T(8,128)(2,1)}, u32[]{:S(2)}) %copy-start) | copy-done | bytes 786456
  44.5 1.1 %copy-done.2 = bf16[3,512,256]{2,1,0:T(8,128)(2,1)S(1)} copy-done((bf16[3,512,256]{2,1,0:T(8,128)(2,1)S(1)}, bf16[3,512,256]{2,1,0:T(8,128)(2,1)}, u32[]{:S(2)}) %copy-start.2) | copy-done | bytes 786456
  46.3 1.5 %collective-permute-start.2 = (f32[2,128,128]{2,1,0:T(8,128)S(1)}, f32[2,128,128]{2,1,0:T(8,128)S(1)}, u32[]{:S(2)}, u32[]{:S(2)}) collective-permute-start(f32[2,128,128]{2,1,0:T(8,128)S(1)} %get-tuple-element.16), channel_id=1, source_target_pairs={{0,128},{64,192},{128,0},{192,64},{1,129},{65,193},{129,1},{193,65... | collective-permute-start | bytes 393224 | tf_op jit(solution)/shard_map/ppermute | solution.py:278
  47.8 3.5 %collective-permute-done.2.crossed_ref = f32[2,128,128]{2,1,0:T(8,128)S(1)} collective-permute-done((f32[2,128,128]{2,1,0:T(8,128)S(1)}, f32[2,128,128]{2,1,0:T(8,128)S(1)}, u32[]{:S(2)}, u32[]{:S(2)}) %collective-permute-start.2) | collective-permute-done | bytes 131104 | tf_op jit(solution)/shard_map/ppermute | solution.py:278
  51.3 1.7 %shard_map.136 = (f32[2,128,128]{2,1,0:T(8,128)S(1)}, f32[256,128]{1,0:T(8,128)}) custom-call(f32[256,128]{1,0:T(8,128)S(1)} %bitcast.11, f32[2,128,128]{2,1,0:T(8,128)S(1)} %copy-done.7, f32[2,128,128]{2,1,0:T(8,128)S(1)} %copy-done.5, s32[2]{0:T(128)S(1)} %copy-done.10, f32[2,128,128]{2,1,0:T(8,128)S(1)} %get-tuple-element.15.base_ref, ...), custom_call_target="tpu_custom_call" | custom-call | bytes 262144 | tf_op jit(solution)/shard_map/pallas_call | solution.py:279
  53.1 12.9 %all-to-all-start.2 = ((f32[64,4,128]{2,1,0:T(4,128)}), f32[64,4,128]{2,1,0:T(4,128)S(1)}, u32[]{:S(2)}, u32[]{:S(2)}) async-start(f32[64,4,128]{2,1,0:T(4,128)} %bitcast.6), calls=%async_computation.2 | async-start | bytes 262144 | tf_op jit(solution)/shard_map/all_to_all | solution.py:231
  66.0 7.7 %collective-permute-start.4 = (f32[2,128,128]{2,1,0:T(8,128)S(1)}, f32[2,128,128]{2,1,0:T(8,128)S(1)}, u32[]{:S(2)}, u32[]{:S(2)}) collective-permute-start(f32[2,128,128]{2,1,0:T(8,128)S(1)} %get-tuple-element.19.own_ref.pressure_ref), channel_id=1, source_target_pairs={{0,63},{1,2},{2,1},{3,4},{4,3},{5,6},{6,5},{7,8},{8,7},{9,10},{10,... | collective-permute-start | bytes 393224 | tf_op jit(solution)/shard_map/ppermute | solution.py:263
  73.7 5.0 %all-to-all-done.2 = f32[64,4,128]{2,1,0:T(4,128)S(1)} async-done(((f32[64,4,128]{2,1,0:T(4,128)}), f32[64,4,128]{2,1,0:T(4,128)S(1)}, u32[]{:S(2)}, u32[]{:S(2)}) %all-to-all-start.2) | async-done | bytes 131104 | tf_op jit(solution)/shard_map/all_to_all | solution.py:231
  78.6 0.8 copy-done.9
  79.4 3.0 %shard_map.137 = f32[256,128]{1,0:T(8,128)} custom-call(f32[256,128]{1,0:T(8,128)S(1)} %bitcast.13, bf16[8,256,256]{2,1,0:T(8,128)(2,1)S(1)} %shard_map.132.ops_ref, f32[64,128]{1,0:T(8,128)S(1)} %copy-done.9), custom_call_target="tpu_custom_call" | custom-call | bytes 262144 | tf_op jit(solution)/shard_map/pallas_call | solution.py:272
  82.4 4.6 %all-to-all-start.3 = ((f32[64,4,128]{2,1,0:T(4,128)}), f32[64,4,128]{2,1,0:T(4,128)S(1)}, u32[]{:S(2)}, u32[]{:S(2)}) async-start(f32[64,4,128]{2,1,0:T(4,128)} %bitcast.8), calls=%async_computation.3 | async-start | bytes 262144 | tf_op jit(solution)/shard_map/all_to_all | solution.py:231
  87.6 1.5 %collective-permute-start.5 = (f32[2,128,128]{2,1,0:T(8,128)S(1)}, f32[2,128,128]{2,1,0:T(8,128)S(1)}, u32[]{:S(2)}, u32[]{:S(2)}) collective-permute-start(f32[2,128,128]{2,1,0:T(8,128)S(1)} %get-tuple-element.21), channel_id=1, source_target_pairs={{0,128},{64,192},{128,0},{192,64},{1,129},{65,193},{129,1},{193,65... | collective-permute-start | bytes 393224 | tf_op jit(solution)/shard_map/ppermute | solution.py:278
  89.1 3.8 %collective-permute-done.5.crossed_ref = f32[2,128,128]{2,1,0:T(8,128)S(1)} collective-permute-done((f32[2,128,128]{2,1,0:T(8,128)S(1)}, f32[2,128,128]{2,1,0:T(8,128)S(1)}, u32[]{:S(2)}, u32[]{:S(2)}) %collective-permute-start.5) | collective-permute-done | bytes 131104 | tf_op jit(solution)/shard_map/ppermute | solution.py:278
  92.9 6.7 %all-to-all-done.3 = f32[64,4,128]{2,1,0:T(4,128)S(1)} async-done(((f32[64,4,128]{2,1,0:T(4,128)}), f32[64,4,128]{2,1,0:T(4,128)S(1)}, u32[]{:S(2)}, u32[]{:S(2)}) %all-to-all-start.3) | async-done | bytes 131104 | tf_op jit(solution)/shard_map/all_to_all | solution.py:231
  99.6 1.5 %shard_map.139 = (f32[2,128,128]{2,1,0:T(8,128)}, f32[2,128,128]{2,1,0:T(8,128)}) custom-call(f32[256,128]{1,0:T(8,128)S(1)} %bitcast.12, f32[2,128,128]{2,1,0:T(8,128)S(1)} %copy-done.7, f32[2,128,128]{2,1,0:T(8,128)S(1)} %copy-done.5, s32[2]{0:T(128)S(1)} %copy-done.10, f32[2,128,128]{2,1,0:T(8,128)S(1)} %get-tuple-element.20.base_ref, ...), custom_call_target="tpu_custom_call" | custom-call | bytes 262144 | tf_op jit(solution)/shard_map/pallas_call | solution.py:279
  (27 shorter events, 1.6 us)
Async XLA Ops:
  2.6 27.8 %all-to-all-start = ((f32[64,5,1,128]{3,2,1,0:T(1,128)}), f32[64,5,1,128]{3,2,1,0:T(1,128)S(1)}, u32[]{:S(2)}, u32[]{:S(2)}) async-start(f32[64,5,1,128]{3,2,1,0:T(1,128)} %bitcast.14), calls=%async_computation | async-start | bytes 327680 | tf_op jit(solution)/shard_map/all_to_all | solution.py:231
  16.2 27.1 %collective-permute-start.1 = (f32[2,128,128]{2,1,0:T(8,128)}, f32[2,128,128]{2,1,0:T(8,128)S(1)}, u32[]{:S(2)}, u32[]{:S(2)}) collective-permute-start(f32[2,128,128]{2,1,0:T(8,128)} %rest_0_.1), channel_id=1, source_target_pairs={{0,63},{1,2},{2,1},{3,4},{4,3},{5,6},{6,5},{7,8},{8,7},{9,10},{10,... | collective-permute-start | bytes 393224 | tf_op jit(solution)/shard_map/ppermute | solution.py:263
  23.9 19.5 %collective-permute-start = (f32[2,128,128]{2,1,0:T(8,128)}, f32[2,128,128]{2,1,0:T(8,128)S(1)}, u32[]{:S(2)}, u32[]{:S(2)}) collective-permute-start(f32[2,128,128]{2,1,0:T(8,128)} %rest_0_.1), channel_id=1, source_target_pairs={{0,1},{1,0},{2,3},{3,2},{4,5},{5,4},{6,7},{7,6},{8,9},{9,8},{10,11... | collective-permute-start | bytes 393224 | tf_op jit(solution)/shard_map/ppermute | solution.py:262
  23.9 1.2 %copy-start.6 = (f32[16,128,128]{2,1,0:T(8,128)S(1)}, f32[16,128,128]{2,1,0:T(8,128)}, u32[]{:S(2)}) copy-start(f32[16,128,128]{2,1,0:T(8,128)} %ops_ref.1) | copy-start | bytes 3145732
  33.4 0.6 copy-start.8
  34.0 17.3 %all-to-all-start.1 = ((f32[64,4,128]{2,1,0:T(4,128)}), f32[64,4,128]{2,1,0:T(4,128)S(1)}, u32[]{:S(2)}, u32[]{:S(2)}) async-start(f32[64,4,128]{2,1,0:T(4,128)} %bitcast.2), calls=%async_computation.1 | async-start | bytes 262144 | tf_op jit(solution)/shard_map/all_to_all | solution.py:231
  38.6 4.8 %copy-start.4 = (f32[2,128,128]{2,1,0:T(8,128)S(1)}, f32[2,128,128]{2,1,0:T(8,128)}, u32[]{:S(2)}) copy-start(f32[2,128,128]{2,1,0:T(8,128)} %rest_0_.1) | copy-start | bytes 393220
  38.6 12.7 %copy-start.5 = (f32[2,128,128]{2,1,0:T(8,128)S(1)}, f32[2,128,128]{2,1,0:T(8,128)}, u32[]{:S(2)}) copy-start(f32[2,128,128]{2,1,0:T(8,128)} %to_moments_ref.5) | copy-start | bytes 393220
  38.6 12.7 %copy-start.7 = (f32[2,128,128]{2,1,0:T(8,128)S(1)}, f32[2,128,128]{2,1,0:T(8,128)}, u32[]{:S(2)}) copy-start(f32[2,128,128]{2,1,0:T(8,128)} %from_locals_ref.3) | copy-start | bytes 393220
  38.7 12.7 %copy-start.10 = (s32[2]{0:T(128)S(1)}, s32[2]{0:T(128)}, u32[]{:S(2)}) copy-start(s32[2]{0:T(128)} %box_ref.5) | copy-start | bytes 28
  43.4 1.1 %copy-start = (bf16[3,512,256]{2,1,0:T(8,128)(2,1)S(1)}, bf16[3,512,256]{2,1,0:T(8,128)(2,1)}, u32[]{:S(2)}) copy-start(bf16[3,512,256]{2,1,0:T(8,128)(2,1)} %get-tuple-element.13.top_ref) | copy-start | bytes 2359300
  44.5 1.1 %copy-start.2 = (bf16[3,512,256]{2,1,0:T(8,128)(2,1)S(1)}, bf16[3,512,256]{2,1,0:T(8,128)(2,1)}, u32[]{:S(2)}) copy-start(bf16[3,512,256]{2,1,0:T(8,128)(2,1)} %get-tuple-element.14.rest_ref) | copy-start | bytes 2359300
  45.7 41.3 %copy-start.1 = (bf16[3,512,256]{2,1,0:T(8,128)(2,1)S(1)}, bf16[3,512,256]{2,1,0:T(8,128)(2,1)}, u32[]{:S(2)}) copy-start(bf16[3,512,256]{2,1,0:T(8,128)(2,1)} %get-tuple-element.13.top_ref) | copy-start | bytes 2359300
  45.7 41.3 %copy-start.3 = (bf16[3,512,256]{2,1,0:T(8,128)(2,1)S(1)}, bf16[3,512,256]{2,1,0:T(8,128)(2,1)}, u32[]{:S(2)}) copy-start(bf16[3,512,256]{2,1,0:T(8,128)(2,1)} %get-tuple-element.14.rest_ref) | copy-start | bytes 2359300
  46.3 5.1 %collective-permute-start.2 = (f32[2,128,128]{2,1,0:T(8,128)S(1)}, f32[2,128,128]{2,1,0:T(8,128)S(1)}, u32[]{:S(2)}, u32[]{:S(2)}) collective-permute-start(f32[2,128,128]{2,1,0:T(8,128)S(1)} %get-tuple-element.16), channel_id=1, source_target_pairs={{0,128},{64,192},{128,0},{192,64},{1,129},{65,193},{129,1},{193,65... | collective-permute-start | bytes 393224 | tf_op jit(solution)/shard_map/ppermute | solution.py:278
  53.1 25.5 %all-to-all-start.2 = ((f32[64,4,128]{2,1,0:T(4,128)}), f32[64,4,128]{2,1,0:T(4,128)S(1)}, u32[]{:S(2)}, u32[]{:S(2)}) async-start(f32[64,4,128]{2,1,0:T(4,128)} %bitcast.6), calls=%async_computation.2 | async-start | bytes 262144 | tf_op jit(solution)/shard_map/all_to_all | solution.py:231
  66.0 21.0 %collective-permute-start.4 = (f32[2,128,128]{2,1,0:T(8,128)S(1)}, f32[2,128,128]{2,1,0:T(8,128)S(1)}, u32[]{:S(2)}, u32[]{:S(2)}) collective-permute-start(f32[2,128,128]{2,1,0:T(8,128)S(1)} %get-tuple-element.19.own_ref.pressure_ref), channel_id=1, source_target_pairs={{0,63},{1,2},{2,1},{3,4},{4,3},{5,6},{6,5},{7,8},{8,7},{9,10},{10,... | collective-permute-start | bytes 393224 | tf_op jit(solution)/shard_map/ppermute | solution.py:263
  73.7 13.3 %collective-permute-start.3 = (f32[2,128,128]{2,1,0:T(8,128)S(1)}, f32[2,128,128]{2,1,0:T(8,128)S(1)}, u32[]{:S(2)}, u32[]{:S(2)}) collective-permute-start(f32[2,128,128]{2,1,0:T(8,128)S(1)} %get-tuple-element.19.own_ref.pressure_ref), channel_id=1, source_target_pairs={{0,1},{1,0},{2,3},{3,2},{4,5},{5,4},{6,7},{7,6},{8,9},{9,8},{10,11... | collective-permute-start | bytes 393224 | tf_op jit(solution)/shard_map/ppermute | solution.py:262
  78.6 0.8 copy-start.9
  82.4 17.3 %all-to-all-start.3 = ((f32[64,4,128]{2,1,0:T(4,128)}), f32[64,4,128]{2,1,0:T(4,128)S(1)}, u32[]{:S(2)}, u32[]{:S(2)}) async-start(f32[64,4,128]{2,1,0:T(4,128)} %bitcast.8), calls=%async_computation.3 | async-start | bytes 262144 | tf_op jit(solution)/shard_map/all_to_all | solution.py:231
  87.6 5.3 %collective-permute-start.5 = (f32[2,128,128]{2,1,0:T(8,128)S(1)}, f32[2,128,128]{2,1,0:T(8,128)S(1)}, u32[]{:S(2)}, u32[]{:S(2)}) collective-permute-start(f32[2,128,128]{2,1,0:T(8,128)S(1)} %get-tuple-element.21), channel_id=1, source_target_pairs={{0,128},{64,192},{128,0},{192,64},{1,129},{65,193},{129,1},{193,65... | collective-permute-start | bytes 393224 | tf_op jit(solution)/shard_map/ppermute | solution.py:278

commit v4 on v3

--- a/solution.py
+++ b/solution.py
@@ -181,7 +181,7 @@
     transfer(in_ref, ops_ref, counts_ref, out_ref, 4)
 
 
-def update_body(last, in_ref, from_locals_ref, to_moments_ref, box_ref, base_ref, crossed_ref, pressure_ref, *outs):
+def update_body(last, in_ref, from_locals_ref, box_ref, base_ref, crossed_ref, pressure_ref, *rest):
     peers = in_ref.shape[0] // 4
     local = []
     for b in range(2):
@@ -192,11 +192,11 @@
         residual = base_ref[c] - (crossed_ref[c] + far)
         field = pressure_ref[c] + DAMPING * residual
         fields.append(field)
-        outs[0][c] = field
+        rest[-2][c] = field
         if last:
-            outs[1][c] = residual
+            rest[-1][c] = residual
     if not last:
-        send_moments(fields, to_moments_ref, box_ref, outs[1], 4)
+        send_moments(fields, rest[0], box_ref, rest[-1], 4)
 
 
 def shards(
@@ -279,10 +279,10 @@
         pressure, sent = call(
             functools.partial(update_body, last),
             (field, field if last else piece),
-            [VMEM] * 3 + [SMEM] + [VMEM] * 3,
+            [VMEM] * 2 + [SMEM] + [VMEM] * (3 if last else 4),
             (VMEM, VMEM),
-            mib=MIB[2],
-        )(local, from_locals, to_moments, cluster_box, base, crossed, pressure)
+            mib=MIB[2] if last else 57,
+        )(local, from_locals, cluster_box, base, crossed, pressure, *(() if last else (to_moments,)))
     return (pressure, sent)
 
 

time: 102 us -> 102 us (level)
    unnamed x22 -> x26, local copies, waits for them, and re-layouts: 4.89 us -> 5.75 us
where the time goes in v4:
time: 102 us
  starting transfers between devices  54.2 us (53%)
  waiting for transfers between devices  23 us (23%)
  Pallas kernels  18 us (18%)
  local copies, waits for them, and re-layouts  5.75 us (6%)
    all_to_all x4, starting transfers between devices, exchange(): lax.all_to_all(x, 'cl', split_axis=0, concat_axis=0, tiled=True)  35.9 us
    all_to_all x4, waiting for transfers between devices, exchange(): lax.all_to_all(x, 'cl', split_axis=0, concat_axis=0, tiled=True)  15.7 us
    ppermute x2, starting transfers between devices, shards(): two = lax.ppermute(pressure, 'cl', second_swap)  15.4 us
    ppermute x2, waiting for transfers between devices, shards(): crossed = lax.ppermute(crossed, 'grp', across)  7.28 us
    unnamed x26, local copies, waits for them, and re-layouts  5.75 us
    pallas_call x1, Pallas kernels, shards(): blocks(near_index, near_count, place, sign, near_real, near_imag)  4.66 us
    pallas_call x2, Pallas kernels, shards(): call(functools.partial(update_body, last), (field, field if last else pie...  3.91 us
    pallas_call x1, Pallas kernels, shards(): call(next_transfer_body, piece, [VMEM] * 3, VMEM, **shared)  2.99 us
  transfers between devices with their start and end apart: 10, of which 5 were waited for; matrix products, arithmetic and copies ran while one was open for 0% of the time, Pallas kernels for 12%

profile of v4, /device:TPU:2, one launch (start us, length us, event | category | flops | bytes accessed | tf_op | source)
XLA Modules:
  0.0 101.7 jit_solution(13062322301447277915)
XLA Ops:
  0.6 1.9 %shard_map.131 = f32[320,128]{1,0:T(8,128)} custom-call(f32[2,128,128]{2,1,0:T(8,128)} %rest_0_.3, f32[2,128,128]{2,1,0:T(8,128)} %rest_0_.2, s32[2,32]{1,0:T(2,128)} %source_ref.1, s32[2,32]{1,0:T(2,128)} %kind_ref.1, s32[2]{0:T(128)} %count_ref.2, s32[2]{0:T(128)} %box_ref.5), custom_call_target="tpu_custom_call" | custom-call | bytes 262144 | tf_op jit(solution)/shard_map/pallas_call | solution.py:247
  2.6 13.7 %all-to-all-start = ((f32[64,5,1,128]{3,2,1,0:T(1,128)}), f32[64,5,1,128]{3,2,1,0:T(1,128)S(1)}, u32[]{:S(2)}, u32[]{:S(2)}) async-start(f32[64,5,1,128]{3,2,1,0:T(1,128)} %bitcast.13), calls=%async_computation | async-start | bytes 327680 | tf_op jit(solution)/shard_map/all_to_all | solution.py:231
  16.2 7.7 %collective-permute-start.1 = (f32[2,128,128]{2,1,0:T(8,128)}, f32[2,128,128]{2,1,0:T(8,128)S(1)}, u32[]{:S(2)}, u32[]{:S(2)}) collective-permute-start(f32[2,128,128]{2,1,0:T(8,128)} %rest_0_.3), channel_id=1, source_target_pairs={{0,63},{1,2},{2,1},{3,4},{4,3},{5,6},{6,5},{7,8},{8,7},{9,10},{10,... | collective-permute-start | bytes 393224 | tf_op jit(solution)/shard_map/ppermute | solution.py:263
  23.9 1.2 %copy-done.6 = f32[16,128,128]{2,1,0:T(8,128)S(1)} copy-done((f32[16,128,128]{2,1,0:T(8,128)S(1)}, f32[16,128,128]{2,1,0:T(8,128)}, u32[]{:S(2)}) %copy-start.6) | copy-done | bytes 1048600
  25.5 4.9 %all-to-all-done = f32[64,5,1,128]{3,2,1,0:T(1,128)S(1)} async-done(((f32[64,5,1,128]{3,2,1,0:T(1,128)}), f32[64,5,1,128]{3,2,1,0:T(1,128)S(1)}, u32[]{:S(2)}, u32[]{:S(2)}) %all-to-all-start) | async-done | bytes 163872 | tf_op jit(solution)/shard_map/all_to_all | solution.py:231
  30.4 3.0 %shard_map.133 = (f32[256,128]{1,0:T(8,128)}, f32[64,128]{1,0:T(8,128)S(1)}) custom-call(f32[320,128]{1,0:T(8,128)S(1)} %bitcast.10, bf16[8,256,256]{2,1,0:T(8,128)(2,1)S(1)} %shard_map.132.ops_ref), custom_call_target="tpu_custom_call" | custom-call | bytes 262144 | tf_op jit(solution)/shard_map/pallas_call | solution.py:268
  33.4 4.6 %all-to-all-start.1 = ((f32[64,4,128]{2,1,0:T(4,128)}), f32[64,4,128]{2,1,0:T(4,128)S(1)}, u32[]{:S(2)}, u32[]{:S(2)}) async-start(f32[64,4,128]{2,1,0:T(4,128)} %bitcast.2), calls=%async_computation.1 | async-start | bytes 262144 | tf_op jit(solution)/shard_map/all_to_all | solution.py:231
  38.0 4.7 %shard_map.134 = (bf16[3,512,256]{2,1,0:T(8,128)(2,1)}, bf16[3,512,256]{2,1,0:T(8,128)(2,1)}) custom-call(s32[2,16]{1,0:T(2,128)} %index_ref.1, s32[2]{0:T(128)} %count_ref.3, s32[1]{0:T(128)} %bitcast.4.place_ref, f32[1]{0:T(128)} %bitcast.5.sign_ref, f32[2,16,128,128]{3,2,1,0:T(8,128)} %real_ref.1, f32[2,16,128,128]{3,2,1,0:T(8,128)} %imag_ref.1), custom_call_target="tpu_custom_call" | custom-call | bytes 262144 | tf_op jit(solution)/shard_map/pallas_call | solution.py:260
  42.7 1.1 %copy-done = bf16[3,512,256]{2,1,0:T(8,128)(2,1)S(1)} copy-done((bf16[3,512,256]{2,1,0:T(8,128)(2,1)S(1)}, bf16[3,512,256]{2,1,0:T(8,128)(2,1)}, u32[]{:S(2)}) %copy-start) | copy-done | bytes 786456
  43.8 1.1 %copy-done.2 = bf16[3,512,256]{2,1,0:T(8,128)(2,1)S(1)} copy-done((bf16[3,512,256]{2,1,0:T(8,128)(2,1)S(1)}, bf16[3,512,256]{2,1,0:T(8,128)(2,1)}, u32[]{:S(2)}) %copy-start.2) | copy-done | bytes 786456
  45.6 0.6 copy-done.9
  46.2 1.4 %collective-permute-start.2 = (f32[2,128,128]{2,1,0:T(8,128)S(1)}, f32[2,128,128]{2,1,0:T(8,128)S(1)}, u32[]{:S(2)}, u32[]{:S(2)}) collective-permute-start(f32[2,128,128]{2,1,0:T(8,128)S(1)} %get-tuple-element.16), channel_id=1, source_target_pairs={{0,128},{64,192},{128,0},{192,64},{1,129},{65,193},{129,1},{193,65... | collective-permute-start | bytes 393224 | tf_op jit(solution)/shard_map/ppermute | solution.py:278
  47.7 3.5 %collective-permute-done.2.crossed_ref = f32[2,128,128]{2,1,0:T(8,128)S(1)} collective-permute-done((f32[2,128,128]{2,1,0:T(8,128)S(1)}, f32[2,128,128]{2,1,0:T(8,128)S(1)}, u32[]{:S(2)}, u32[]{:S(2)}) %collective-permute-start.2) | collective-permute-done | bytes 131104 | tf_op jit(solution)/shard_map/ppermute | solution.py:278
  51.9 2.4 %shard_map.136 = (f32[2,128,128]{2,1,0:T(8,128)}, f32[256,128]{1,0:T(8,128)}) custom-call(f32[256,128]{1,0:T(8,128)} %bitcast.14, f32[2,128,128]{2,1,0:T(8,128)} %from_locals_ref.3, s32[2]{0:T(128)} %box_ref.5, f32[2,128,128]{2,1,0:T(8,128)} %copy-done.9, f32[2,128,128]{2,1,0:T(8,128)} %copy-done.12, f32[2,128,128]{2,1,0:T(8,128)} %rest_0_.3, ...), custom_call_target="tpu_custom_call" | custom-call | bytes 262144 | tf_op jit(solution)/shard_map/pallas_call | solution.py:279
  54.3 13.0 %all-to-all-start.2 = ((f32[64,4,128]{2,1,0:T(4,128)}), f32[64,4,128]{2,1,0:T(4,128)S(1)}, u32[]{:S(2)}, u32[]{:S(2)}) async-start(f32[64,4,128]{2,1,0:T(4,128)} %bitcast.15), calls=%async_computation.2 | async-start | bytes 262144 | tf_op jit(solution)/shard_map/all_to_all | solution.py:231
  67.3 7.7 %collective-permute-start.4 = (f32[2,128,128]{2,1,0:T(8,128)}, f32[2,128,128]{2,1,0:T(8,128)S(1)}, u32[]{:S(2)}, u32[]{:S(2)}) collective-permute-start(f32[2,128,128]{2,1,0:T(8,128)} %get-tuple-element.19.own_ref.pressure_ref), channel_id=1, source_target_pairs={{0,63},{1,2},{2,1},{3,4},{4,3},{5,6},{6,5},{7,8},{8,7},{9,10},{10,... | collective-permute-start | bytes 393224 | tf_op jit(solution)/shard_map/ppermute | solution.py:263
  75.0 4.9 %all-to-all-done.2 = f32[64,4,128]{2,1,0:T(4,128)S(1)} async-done(((f32[64,4,128]{2,1,0:T(4,128)}), f32[64,4,128]{2,1,0:T(4,128)S(1)}, u32[]{:S(2)}, u32[]{:S(2)}) %all-to-all-start.2) | async-done | bytes 131104 | tf_op jit(solution)/shard_map/all_to_all | solution.py:231
  79.9 3.0 %shard_map.137 = f32[256,128]{1,0:T(8,128)} custom-call(f32[256,128]{1,0:T(8,128)S(1)} %bitcast.12, bf16[8,256,256]{2,1,0:T(8,128)(2,1)S(1)} %shard_map.132.ops_ref, f32[64,128]{1,0:T(8,128)S(1)} %get-tuple-element.18.lists_ref), custom_call_target="tpu_custom_call" | custom-call | bytes 262144 | tf_op jit(solution)/shard_map/pallas_call | solution.py:272
  82.9 4.6 %all-to-all-start.3 = ((f32[64,4,128]{2,1,0:T(4,128)}), f32[64,4,128]{2,1,0:T(4,128)S(1)}, u32[]{:S(2)}, u32[]{:S(2)}) async-start(f32[64,4,128]{2,1,0:T(4,128)} %bitcast.8), calls=%async_computation.3 | async-start | bytes 262144 | tf_op jit(solution)/shard_map/all_to_all | solution.py:231
  87.6 0.9 copy-done.7
  89.1 1.5 %collective-permute-start.5 = (f32[2,128,128]{2,1,0:T(8,128)S(1)}, f32[2,128,128]{2,1,0:T(8,128)S(1)}, u32[]{:S(2)}, u32[]{:S(2)}) collective-permute-start(f32[2,128,128]{2,1,0:T(8,128)S(1)} %get-tuple-element.21), channel_id=1, source_target_pairs={{0,128},{64,192},{128,0},{192,64},{1,129},{65,193},{129,1},{193,65... | collective-permute-start | bytes 393224 | tf_op jit(solution)/shard_map/ppermute | solution.py:278
  90.6 3.7 %collective-permute-done.5.crossed_ref = f32[2,128,128]{2,1,0:T(8,128)S(1)} collective-permute-done((f32[2,128,128]{2,1,0:T(8,128)S(1)}, f32[2,128,128]{2,1,0:T(8,128)S(1)}, u32[]{:S(2)}, u32[]{:S(2)}) %collective-permute-start.5) | collective-permute-done | bytes 131104 | tf_op jit(solution)/shard_map/ppermute | solution.py:278
  94.4 5.8 %all-to-all-done.3 = f32[64,4,128]{2,1,0:T(4,128)S(1)} async-done(((f32[64,4,128]{2,1,0:T(4,128)}), f32[64,4,128]{2,1,0:T(4,128)S(1)}, u32[]{:S(2)}, u32[]{:S(2)}) %all-to-all-start.3) | async-done | bytes 131104 | tf_op jit(solution)/shard_map/all_to_all | solution.py:231
  100.2 1.5 %shard_map.139 = (f32[2,128,128]{2,1,0:T(8,128)}, f32[2,128,128]{2,1,0:T(8,128)}) custom-call(f32[256,128]{1,0:T(8,128)S(1)} %bitcast.11, f32[2,128,128]{2,1,0:T(8,128)S(1)} %copy-done.8, s32[2]{0:T(128)S(1)} %copy-done.10, f32[2,128,128]{2,1,0:T(8,128)S(1)} %get-tuple-element.20.base_ref, f32[2,128,128]{2,1,0:T(8,128)S(1)} %collective-permute-done.5.crossed_ref, ...), custom_call_target="tpu_custom_call" | custom-call | bytes 262144 | tf_op jit(solution)/shard_map/pallas_call | solution.py:279
  (31 shorter events, 2.2 us)
Async XLA Ops:
  2.6 27.8 %all-to-all-start = ((f32[64,5,1,128]{3,2,1,0:T(1,128)}), f32[64,5,1,128]{3,2,1,0:T(1,128)S(1)}, u32[]{:S(2)}, u32[]{:S(2)}) async-start(f32[64,5,1,128]{3,2,1,0:T(1,128)} %bitcast.13), calls=%async_computation | async-start | bytes 327680 | tf_op jit(solution)/shard_map/all_to_all | solution.py:231
  16.2 26.4 %collective-permute-start.1 = (f32[2,128,128]{2,1,0:T(8,128)}, f32[2,128,128]{2,1,0:T(8,128)S(1)}, u32[]{:S(2)}, u32[]{:S(2)}) collective-permute-start(f32[2,128,128]{2,1,0:T(8,128)} %rest_0_.3), channel_id=1, source_target_pairs={{0,63},{1,2},{2,1},{3,4},{4,3},{5,6},{6,5},{7,8},{8,7},{9,10},{10,... | collective-permute-start | bytes 393224 | tf_op jit(solution)/shard_map/ppermute | solution.py:263
  23.9 18.7 %collective-permute-start = (f32[2,128,128]{2,1,0:T(8,128)}, f32[2,128,128]{2,1,0:T(8,128)S(1)}, u32[]{:S(2)}, u32[]{:S(2)}) collective-permute-start(f32[2,128,128]{2,1,0:T(8,128)} %rest_0_.3), channel_id=1, source_target_pairs={{0,1},{1,0},{2,3},{3,2},{4,5},{5,4},{6,7},{7,6},{8,9},{9,8},{10,11... | collective-permute-start | bytes 393224 | tf_op jit(solution)/shard_map/ppermute | solution.py:262
  23.9 1.2 %copy-start.6 = (f32[16,128,128]{2,1,0:T(8,128)S(1)}, f32[16,128,128]{2,1,0:T(8,128)}, u32[]{:S(2)}) copy-start(f32[16,128,128]{2,1,0:T(8,128)} %ops_ref.1) | copy-start | bytes 3145732
  33.4 17.8 %all-to-all-start.1 = ((f32[64,4,128]{2,1,0:T(4,128)}), f32[64,4,128]{2,1,0:T(4,128)S(1)}, u32[]{:S(2)}, u32[]{:S(2)}) async-start(f32[64,4,128]{2,1,0:T(4,128)} %bitcast.2), calls=%async_computation.1 | async-start | bytes 262144 | tf_op jit(solution)/shard_map/all_to_all | solution.py:231
  38.0 4.7 %copy-start.4 = (f32[2,128,128]{2,1,0:T(8,128)S(1)}, f32[2,128,128]{2,1,0:T(8,128)}, u32[]{:S(2)}) copy-start(f32[2,128,128]{2,1,0:T(8,128)} %rest_0_.3) | copy-start | bytes 393220
  42.7 1.1 %copy-start = (bf16[3,512,256]{2,1,0:T(8,128)(2,1)S(1)}, bf16[3,512,256]{2,1,0:T(8,128)(2,1)}, u32[]{:S(2)}) copy-start(bf16[3,512,256]{2,1,0:T(8,128)(2,1)} %get-tuple-element.13.top_ref) | copy-start | bytes 2359300
  43.8 1.1 %copy-start.2 = (bf16[3,512,256]{2,1,0:T(8,128)(2,1)S(1)}, bf16[3,512,256]{2,1,0:T(8,128)(2,1)}, u32[]{:S(2)}) copy-start(bf16[3,512,256]{2,1,0:T(8,128)(2,1)} %get-tuple-element.14.rest_ref) | copy-start | bytes 2359300
  45.0 42.6 %copy-start.1 = (bf16[3,512,256]{2,1,0:T(8,128)(2,1)S(1)}, bf16[3,512,256]{2,1,0:T(8,128)(2,1)}, u32[]{:S(2)}) copy-start(bf16[3,512,256]{2,1,0:T(8,128)(2,1)} %get-tuple-element.13.top_ref) | copy-start | bytes 2359300
  45.0 42.6 %copy-start.3 = (bf16[3,512,256]{2,1,0:T(8,128)(2,1)S(1)}, bf16[3,512,256]{2,1,0:T(8,128)(2,1)}, u32[]{:S(2)}) copy-start(bf16[3,512,256]{2,1,0:T(8,128)(2,1)} %get-tuple-element.14.rest_ref) | copy-start | bytes 2359300
  45.0 42.6 %copy-start.5 = (f32[2,128,128]{2,1,0:T(8,128)S(1)}, f32[2,128,128]{2,1,0:T(8,128)}, u32[]{:S(2)}) copy-start(f32[2,128,128]{2,1,0:T(8,128)} %rest_0_.3) | copy-start | bytes 393220
  45.6 0.7 copy-start.9
  46.2 5.0 %collective-permute-start.2 = (f32[2,128,128]{2,1,0:T(8,128)S(1)}, f32[2,128,128]{2,1,0:T(8,128)S(1)}, u32[]{:S(2)}, u32[]{:S(2)}) collective-permute-start(f32[2,128,128]{2,1,0:T(8,128)S(1)} %get-tuple-element.16), channel_id=1, source_target_pairs={{0,128},{64,192},{128,0},{192,64},{1,129},{65,193},{129,1},{193,65... | collective-permute-start | bytes 393224 | tf_op jit(solution)/shard_map/ppermute | solution.py:278
  51.2 0.6 copy-start.12
  51.2 0.7 copy-start.11
  54.3 45.9 %copy-start.8 = (f32[2,128,128]{2,1,0:T(8,128)S(1)}, f32[2,128,128]{2,1,0:T(8,128)}, u32[]{:S(2)}) copy-start(f32[2,128,128]{2,1,0:T(8,128)} %from_locals_ref.3) | copy-start | bytes 393220
  54.3 45.9 %copy-start.10 = (s32[2]{0:T(128)S(1)}, s32[2]{0:T(128)}, u32[]{:S(2)}) copy-start(s32[2]{0:T(128)} %box_ref.5) | copy-start | bytes 28
  54.3 25.6 %all-to-all-start.2 = ((f32[64,4,128]{2,1,0:T(4,128)}), f32[64,4,128]{2,1,0:T(4,128)S(1)}, u32[]{:S(2)}, u32[]{:S(2)}) async-start(f32[64,4,128]{2,1,0:T(4,128)} %bitcast.15), calls=%async_computation.2 | async-start | bytes 262144 | tf_op jit(solution)/shard_map/all_to_all | solution.py:231
  67.3 20.3 %collective-permute-start.4 = (f32[2,128,128]{2,1,0:T(8,128)}, f32[2,128,128]{2,1,0:T(8,128)S(1)}, u32[]{:S(2)}, u32[]{:S(2)}) collective-permute-start(f32[2,128,128]{2,1,0:T(8,128)} %get-tuple-element.19.own_ref.pressure_ref), channel_id=1, source_target_pairs={{0,63},{1,2},{2,1},{3,4},{4,3},{5,6},{6,5},{7,8},{8,7},{9,10},{10,... | collective-permute-start | bytes 393224 | tf_op jit(solution)/shard_map/ppermute | solution.py:263
  75.0 12.6 %collective-permute-start.3 = (f32[2,128,128]{2,1,0:T(8,128)}, f32[2,128,128]{2,1,0:T(8,128)S(1)}, u32[]{:S(2)}, u32[]{:S(2)}) collective-permute-start(f32[2,128,128]{2,1,0:T(8,128)} %get-tuple-element.19.own_ref.pressure_ref), channel_id=1, source_target_pairs={{0,1},{1,0},{2,3},{3,2},{4,5},{5,4},{6,7},{7,6},{8,9},{9,8},{10,11... | collective-permute-start | bytes 393224 | tf_op jit(solution)/shard_map/ppermute | solution.py:262
  82.9 17.3 %all-to-all-start.3 = ((f32[64,4,128]{2,1,0:T(4,128)}), f32[64,4,128]{2,1,0:T(4,128)S(1)}, u32[]{:S(2)}, u32[]{:S(2)}) async-start(f32[64,4,128]{2,1,0:T(4,128)} %bitcast.8), calls=%async_computation.3 | async-start | bytes 262144 | tf_op jit(solution)/shard_map/all_to_all | solution.py:231
  87.6 0.9 copy-start.7
  89.1 5.3 %collective-permute-start.5 = (f32[2,128,128]{2,1,0:T(8,128)S(1)}, f32[2,128,128]{2,1,0:T(8,128)S(1)}, u32[]{:S(2)}, u32[]{:S(2)}) collective-permute-start(f32[2,128,128]{2,1,0:T(8,128)S(1)} %get-tuple-element.21), channel_id=1, source_target_pairs={{0,128},{64,192},{128,0},{192,64},{1,129},{65,193},{129,1},{193,65... | collective-permute-start | bytes 393224 | tf_op jit(solution)/shard_map/ppermute | solution.py:278
